TPU v7x, 32 devices: a whole 2x2x4 slice. The times are simulated.
32 devices in a mesh: band: 4 (over y, x), img: 8 (over z, core).
Axes of the slice: x: 2, y: 2, z: 4, core: 2. Of those that a mesh axis runs over, the one named last changes fastest.
Arguments:
- images: bfloat16 [4, 128, 3328], P('band', 'img'), may hold values from -12 to 12
- references: bfloat16 [4, 32, 3328], P('band', 'img'), may hold values from -0.08 to 0.08
- noise_weight: float32 [4, 1664], P('band'), may hold values from 0.5 to 4
- masks: int32 [4, 16, 8, 49], P('band', 'img'), may hold values from 0 to 1, as said below
Outputs:
- weighted_sums: float32 [4, 32, 3328], P('band', 'img')
- weight_totals: float32 [32], P('img')
Inputs may be any that keep to these rules, and one draw needn't show every extreme that they name: `masks`: each entry is 0 or 1; translation number 49 // 2 is kept in every band, image block and orientation block.
All inputs are finite; a program needn't handle non-finite values.
Results may differ from a plain program's by a relative error of at most 0.0065.
Values may be sent and summed in bfloat16 or wider, within the bound.
No kernel may reach another device: no remote copies, remote signals or barrier semaphores. Data moves between devices by JAX's collectives and lax.ppermute only.
A program may use at most 64 MiB of HBM per device.

v0:
```python
import functools
import math

import jax
import jax.numpy as jnp
from jax import lax
from jax.experimental import pallas as pl
from jax.experimental.pallas import tpu as pltpu
from jax.sharding import PartitionSpec as P


BOX = 256
PENALTY = 10000.0
LANES = 128
NEG = -3.0e38


F32 = jnp.float32
BF16 = jnp.bfloat16


def round_up(value, step):
    return -(-value // step) * step


def dot(a, b, dims):
    return lax.dot_general(a, b, (dims, ((), ())), preferred_element_type=F32)


def prepare_kernel(side, pair, slots, axes, given, other, other_mask, results, scratch):
    rotated, cosine, sine, dropped, own_refs, own_weight = results
    own, own_mask, sems = scratch
    owned = own_refs.shape[0]
    copies = []
    for number, (source, target) in enumerate(zip(given, (own, own_mask, own_refs, own_weight))):
        copies.append(pltpu.make_async_copy(source, target, sems.at[number]))
        copies[-1].start()
    half = side // 2
    coef = cosine.shape[1]
    band = lax.axis_index(axes[0])
    place = lax.axis_index(axes[1])

    shape = (8, coef)
    row = lax.broadcasted_iota(jnp.int32, shape, 0)
    index = lax.broadcasted_iota(jnp.int32, shape, 1)

    def modulo(value, period):
        count = jnp.floor((value.astype(F32) + 0.5) * (1.0 / period)).astype(jnp.int32)
        return value - count * period

    freq_x = modulo(index * 37 + band * 11, 257) - 128
    freq_y = modulo(index * 61 + band * 29, 129)
    phase = jnp.where(row < half, (row + 1) * freq_x, (row - half + 1) * freq_y)
    phase = jnp.bitwise_and(phase + BOX // 2, BOX - 1) - BOX // 2
    angle = phase.astype(F32) * (2.0 * math.pi / BOX)
    cosine[...] = jnp.cos(angle)
    sine[...] = jnp.sin(angle)

    copies[0].wait()
    count = own.shape[0]
    total = pair * count
    for part, source in enumerate((own, other)[:pair]):
        for start in range(0, coef, LANES):
            lanes, far = pl.ds(start, LANES), pl.ds(coef + start, LANES)

            def put(step, real, imag):
                rows = pl.ds((step + half) * total + part * count, count)
                rotated[rows, lanes] = real.astype(BF16)
                rotated[rows, far] = imag.astype(BF16)

            rotated[pl.ds(half * total + part * count, count), lanes] = source[:, lanes]
            rotated[pl.ds(half * total + part * count, count), far] = source[:, far]
            real = source[:, lanes].astype(F32)
            imag = source[:, far].astype(F32)
            for step in range(1, half + 1):
                c = cosine[step - 1 : step, lanes]
                s = sine[step - 1 : step, lanes]
                rc, rs, ic, iss = real * c, real * s, imag * c, imag * s
                put(step, rc - iss, rs + ic)
                put(-step, rc + iss, ic - rs)

    copies[1].wait()
    blocks, owners, shifts = own_mask.shape
    orient = slots * owned
    wide = dropped.shape[1]
    kept = own_mask[...].reshape(blocks * owners, shifts)
    if pair > 1:
        kept = jnp.concatenate([kept, other_mask[...].reshape(blocks * owners, shifts)], axis=0)
    gone = (1 - kept).astype(F32).astype(BF16)
    rows = kept.shape[0]
    column = lax.broadcasted_iota(jnp.int32, (shifts, wide), 1)
    shift = lax.broadcasted_iota(jnp.int32, (shifts, wide), 0)
    move_y = column // orient
    column_r = lax.broadcasted_iota(jnp.int32, (rows, wide), 1)
    row_r = lax.broadcasted_iota(jnp.int32, (rows, wide), 0)
    slot = (column_r % orient) // owned
    owner = jnp.bitwise_xor(slot, place // pair) * pair + place % pair
    mine = (row_r % owners == owner) & (column_r < side * orient)
    per_block = count // blocks
    spread = (
        lax.broadcasted_iota(jnp.int32, (total, rows), 0) // per_block
        == lax.broadcasted_iota(jnp.int32, (total, rows), 1) // owners
    )
    spread = spread.astype(F32).astype(BF16)
    for step in range(side):
        pick = ((shift == step * side + move_y) & (move_y < side)).astype(F32).astype(BF16)
        chosen = jnp.where(mine, dot(gone, pick, ((1,), (0,))), 0.0).astype(BF16)
        dropped[pl.ds(step * total, total), :] = PENALTY * dot(spread, chosen, ((1,), (0,)))
    copies[2].wait()
    copies[3].wait()


def score_kernel(side, slots, weight, rotated, cosine, sine, dropped, *rest):
    blocks, (partial, stacked, turned) = rest[:slots], rest[slots:]
    half = side // 2
    coef = cosine.shape[1]
    owned = blocks[0].shape[0]
    orient = slots * owned
    wide = partial.shape[1]
    for slot in range(slots):
        stacked[pl.ds(slot * owned, owned), :] = blocks[slot][...].astype(F32)
    if wide > side * orient:
        rest_rows = pl.ds(side * orient, wide - side * orient)
        turned[rest_rows, :] = jnp.zeros((wide - side * orient, 2 * coef), BF16)
    norms = jnp.zeros((orient, LANES), F32)
    for start in range(0, coef, LANES):
        lanes, far = pl.ds(start, LANES), pl.ds(coef + start, LANES)
        scale = weight[:, lanes]
        real, imag = stacked[:, lanes], stacked[:, far]
        norms = norms + (real * real + imag * imag) * scale
        real = (real * scale).astype(BF16)
        imag = (imag * scale).astype(BF16)

        def put(step, a, b):
            rows = pl.ds((step + half) * orient, orient)
            turned[rows, lanes] = a.astype(BF16)
            turned[rows, far] = b.astype(BF16)

        put(0, real, imag)
        real, imag = real.astype(F32), imag.astype(F32)
        for step in range(1, half + 1):
            c = cosine[half + step - 1 : half + step, lanes]
            s = sine[half + step - 1 : half + step, lanes]
            rc, rs, ic, iss = real * c, real * s, imag * c, imag * s
            put(step, rc + iss, ic - rs)
            put(-step, rc - iss, ic + rs)
    norms = jnp.sum(norms, axis=1, keepdims=True)
    column = lax.broadcasted_iota(jnp.int32, (orient, wide), 1)
    row = lax.broadcasted_iota(jnp.int32, (orient, wide), 0)
    same = (column % orient == row) & (column < side * orient)
    level = jnp.sum(jnp.where(same, norms, 0.0), axis=0, keepdims=True)
    cross = dot(rotated[...], turned[...], ((1,), (1,)))
    partial[...] = cross - 0.5 * level - dropped[...]


def tree_sum(values):
    while len(values) > 1:
        values = [a + b for a, b in zip(values[0::2], values[1::2])]
    return values[0]


def raise_kernel(side, used, *refs):
    parts, (raised, stats) = refs[:-2], refs[-2:]
    score = tree_sum([part[...] for part in parts])
    rows, wide = score.shape
    total = rows // side
    lane = lax.broadcasted_iota(jnp.int32, (rows, wide), 1)
    score = jnp.where(lane < used, score, NEG)
    peak = score[:total]
    for step in range(1, side):
        peak = jnp.maximum(peak, score[step * total : (step + 1) * total])
    peak = jnp.max(peak, axis=1, keepdims=True)
    added = jnp.zeros((total, wide), F32)
    for step in range(side):
        value = jnp.exp(score[step * total : (step + 1) * total] - peak)
        raised[pl.ds(step * total, total), :] = value
        added = added + value
    mass = jnp.sum(added, axis=1, keepdims=True)
    place = lax.broadcasted_iota(jnp.int32, stats.shape, 1)
    stats[...] = jnp.where(place == 0, peak, jnp.where(place == 1, mass, 0.0))


def sum_kernel(side, slots, pair, raised, own_stats, other_stats, rotated, cosine, sine, *rest):
    own_sums, own_mass, messages, moved = rest[0], rest[1], rest[2 : 1 + slots], rest[1 + slots]
    half = side // 2
    coef = cosine.shape[1]
    rows, wide = raised.shape
    total = rows // side
    owned = own_sums.shape[0]
    orient = slots * owned
    peak, mass = own_stats[:, 0:1], own_stats[:, 1:2]
    if pair > 1:
        count = total // pair
        swapped = jnp.concatenate([other_stats[count:, :], other_stats[:count, :]], axis=0)
        top = jnp.maximum(peak, swapped[:, 0:1])
        factor = jnp.exp(peak - top)
        whole = mass * factor + swapped[:, 1:2] * jnp.exp(swapped[:, 0:1] - top)
        factor = factor / whole
    else:
        factor = 1.0 / mass
    posts = []
    columns = jnp.zeros((total, wide), F32)
    for step in range(side):
        prob = raised[pl.ds(step * total, total), :] * factor
        columns = columns + prob
        posts.append(prob.astype(BF16))
    post = jnp.concatenate(posts, axis=0)
    columns = jnp.sum(columns, axis=0, keepdims=True)
    column = lax.broadcasted_iota(jnp.int32, (orient, wide), 1)
    row = lax.broadcasted_iota(jnp.int32, (orient, wide), 0)
    same = (column % orient == row) & (column < side * orient)
    masses = jnp.sum(jnp.where(same, columns, 0.0), axis=1, keepdims=True)
    spread = jnp.broadcast_to(masses, (orient, LANES))
    high = spread.astype(BF16)
    low = (spread - high.astype(F32)).astype(BF16)
    lane = lax.broadcasted_iota(jnp.int32, (orient, LANES), 1)
    tail = jnp.where(lane == 0, high.astype(F32), jnp.where(lane == 1, low.astype(F32), 0.0))
    own_mass[...] = spread[:owned]
    for slot in range(1, slots):
        piece = tail[slot * owned : (slot + 1) * owned]
        messages[slot - 1][:, pl.ds(2 * coef, LANES)] = piece.astype(BF16)

    moved[...] = dot(post, rotated[...], ((0,), (0,)))
    for start in range(0, coef, LANES):
        lanes, far = pl.ds(start, LANES), pl.ds(coef + start, LANES)

        def take(step, where):
            return moved[pl.ds((step + half) * orient, orient), where]

        real, imag = take(0, lanes), take(0, far)
        for step in range(1, half + 1):
            c = cosine[half + step - 1 : half + step, lanes]
            s = sine[half + step - 1 : half + step, lanes]
            ra, rb = take(step, lanes), take(-step, lanes)
            ia, ib = take(step, far), take(-step, far)
            real = real + (ra + rb) * c - (ia - ib) * s
            imag = imag + (ia + ib) * c + (ra - rb) * s
        own_sums[:, lanes] = real[:owned]
        own_sums[:, far] = imag[:owned]
        for slot in range(1, slots):
            part = slice(slot * owned, (slot + 1) * owned)
            messages[slot - 1][:, lanes] = real[part].astype(BF16)
            messages[slot - 1][:, far] = imag[part].astype(BF16)


def finish_kernel(own_sums, own_mass, *rest):
    messages, (sums, mass) = rest[:-2], rest[-2:]
    wide = sums.shape[1]
    owned = sums.shape[0]
    out = own_sums[...]
    level = own_mass[:, 0:1]
    for message in messages:
        out = out + message[:, pl.ds(0, wide)].astype(F32)
        tail = message[:, pl.ds(wide, LANES)].astype(F32)
        level = level + (tail[:, 0:1] + tail[:, 1:2])
    sums[...] = out
    row = lax.broadcasted_iota(jnp.int32, (owned, LANES), 0)
    lane = lax.broadcasted_iota(jnp.int32, (owned, LANES), 1)
    line = jnp.sum(jnp.where(row == lane, level, 0.0), axis=0, keepdims=True)
    mass[...] = line[:, :owned]


def call(kernel, outs, scratch=(), far=0):
    def size(value):
        return math.prod(value.shape) * jnp.dtype(value.dtype).itemsize

    def run(*args):
        held = [*args, *jax.tree.leaves(outs), *[value for value in scratch if value.memory_space == pltpu.MemorySpace.VMEM]]
        grant = 2 * sum(size(value) for value in held) + 4 * 1024 * 1024
        spaces = [pltpu.MemorySpace.HBM] * far + [pltpu.MemorySpace.VMEM] * (len(args) - far)
        return pl.pallas_call(
            kernel,
            in_specs=[pl.BlockSpec(memory_space=space) for space in spaces],
            out_shape=outs,
            scratch_shapes=list(scratch),
            compiler_params=pltpu.CompilerParams(vmem_limit_bytes=min(grant, 60 * 1024 * 1024)),
        )(*args)

    return run


def shaped(shape, dtype):
    return jax.ShapeDtypeStruct(shape, dtype)


def per_device(bands, places, images, references, noise_weight, masks):
    images, references, masks = images[0], references[0], masks[0]
    pair = 2 if places % 2 == 0 else 1
    slots = places // pair
    owned = references.shape[0]
    coef = noise_weight.shape[1]
    count = images.shape[0]
    side = math.isqrt(masks.shape[2])
    total = count * pair
    orient = slots * owned
    used = side * orient
    wide = round_up(used, LANES)

    def across(value, axis, size, step):
        return lax.ppermute(value, axis, [(i, i ^ step) for i in range(size)])

    far_first = list(range(slots - 1, 0, -1))
    blocks = {}
    if pair > 1:
        other = across(images, "img", places, 1)
        other_masks = across(masks, "img", places, 1)
    else:
        other, other_masks = images, masks
    for slot in far_first:
        blocks[slot] = across(references, "img", places, slot * pair)

    def prepare(*refs):
        given, refs = refs[:4], refs[4:]
        prepare_kernel(side, pair, slots, ("band", "img"), given, refs[0], refs[1], refs[2:8], refs[8:])

    rotated, cosine, sine, dropped, blocks[0], weight = call(
        prepare,
        (
            shaped((side * total, 2 * coef), BF16),
            shaped((8, coef), F32),
            shaped((8, coef), F32),
            shaped((side * total, wide), F32),
            shaped(references.shape, references.dtype),
            shaped(noise_weight.shape, noise_weight.dtype),
        ),
        (
            pltpu.VMEM(images.shape, images.dtype),
            pltpu.VMEM(masks.shape, masks.dtype),
            pltpu.SemaphoreType.DMA((4,)),
        ),
        4,
    )(*[pltpu.with_memory_space_constraint(value, pltpu.MemorySpace.HBM) for value in (images, masks, references, noise_weight)], other, other_masks)

    partial = call(
        functools.partial(score_kernel, side, slots),
        shaped((side * total, wide), F32),
        (pltpu.VMEM((orient, 2 * coef), F32), pltpu.VMEM((wide, 2 * coef), BF16)),
    )(weight, rotated, cosine, sine, dropped, *[blocks[slot] for slot in range(slots)])

    parts = {0: partial}
    for step in range(bands - 1, 0, -1):
        parts[step] = across(partial, "band", bands, step)
    raised, stats = call(
        functools.partial(raise_kernel, side, used),
        (shaped((side * total, wide), F32), shaped((total, LANES), F32)),
    )(*[parts[step] for step in range(bands)])
    other_stats = across(stats, "img", places, 1) if pair > 1 else stats

    outs = call(
        functools.partial(sum_kernel, side, slots, pair),
        (shaped((owned, 2 * coef), F32), shaped((owned, LANES), F32))
        + (shaped((owned, 2 * coef + LANES), BF16),) * (slots - 1),
        (pltpu.VMEM((wide, 2 * coef), F32),),
    )(raised, stats, other_stats, rotated, cosine, sine)
    own_sums, own_mass, messages = outs[0], outs[1], outs[2:]
    arrived = {}
    for slot in far_first:
        arrived[slot] = across(messages[slot - 1], "img", places, slot * pair)
    sums, mass = call(
        finish_kernel, (shaped((owned, 2 * coef), F32), shaped((1, owned), F32))
    )(own_sums, own_mass, *[arrived[slot] for slot in range(1, slots)])
    return sums[None], mass[0]


def solution(mesh):
    bands, places = mesh.shape["band"], mesh.shape["img"]
    in_specs = (
        P("band", "img", None),
        P("band", "img", None),
        P("band", None),
        P("band", "img", None, None),
    )
    out_specs = (P("band", "img", None), P("img"))

    def body(*args):
        return per_device(bands, places, *args)

    return jax.shard_map(body, mesh=mesh, in_specs=in_specs, out_specs=out_specs, check_vma=False)
```

profile of v0, /device:TPU:0, one launch (start us, length us, event | category | flops | bytes accessed | tf_op | source)
XLA Modules:
  0.0 32.4 jit_solution(6455086837719920644)
XLA Ops:
  0.6 0.6 %collective-permute-start = (bf16[16,3328]{1,0:T(8,128)(2,1)}, bf16[16,3328]{1,0:T(8,128)(2,1)S(1)}, u32[]{:S(2)}, u32[]{:S(2)}) collective-permute-start(bf16[16,3328]{1,0:T(8,128)(2,1)} %bitcast.5), channel_id=1, source_target_pairs={{0,1},{1,0},{2,3},{3,2},{4,5},{5,4},{6,7},{7,6},{8,9},{9,8},{10,11... | collective-permute-start | bytes 319496 | tf_op jit(solution)/shard_map/ppermute | solution.py:300
  1.2 4.7 %collective-permute-start.4 = (bf16[4,3328]{1,0:T(4,128)(2,1)}, bf16[4,3328]{1,0:T(4,128)(2,1)S(1)}, u32[]{:S(2)}, u32[]{:S(2)}) collective-permute-start(bf16[4,3328]{1,0:T(4,128)(2,1)} %bitcast.7), channel_id=1, source_target_pairs={{0,6},{1,7},{2,4},{3,5},{4,2},{5,3},{6,0},{7,1},{8,14},{9,15},{10,... | collective-permute-start | bytes 79880 | tf_op jit(solution)/shard_map/ppermute | solution.py:300
  5.9 0.0 collective-permute-start.3
  5.9 0.6 %collective-permute-start.2 = (bf16[4,3328]{1,0:T(4,128)(2,1)}, bf16[4,3328]{1,0:T(4,128)(2,1)S(1)}, u32[]{:S(2)}, u32[]{:S(2)}) collective-permute-start(bf16[4,3328]{1,0:T(4,128)(2,1)} %bitcast.9), channel_id=1, source_target_pairs={{0,2},{1,3},{2,0},{3,1},{4,6},{5,7},{6,4},{7,5},{8,10},{9,11},{10,... | collective-permute-start | bytes 79880 | tf_op jit(solution)/shard_map/ppermute | solution.py:300
  6.5 1.4 %collective-permute-done.1.refs_5_ = s32[2,8,49]{2,1,0:T(8,128)S(1)} collective-permute-done((s32[2,8,49]{2,1,0:T(8,128)}, s32[2,8,49]{2,1,0:T(8,128)S(1)}, u32[]{:S(2)}, u32[]{:S(2)}) %collective-permute-start.1) | collective-permute-done | bytes 3168 | tf_op jit(solution)/shard_map/ppermute | solution.py:300
  7.9 2.3 %shard_map.59 = (bf16[224,3328]{1,0:T(8,128)(2,1)S(1)}, f32[8,1664]{1,0:T(8,128)S(1)}, f32[8,1664]{1,0:T(8,128)S(1)}, f32[224,128]{1,0:T(8,128)S(1)}, bf16[4,332...) custom-call(bf16[16,3328]{1,0:T(8,128)(2,1)} %bitcast.6, s32[2,8,49]{2,1,0:T(8,128)} %bitcast.12, bf16[4,3328]{1,0:T(4,128)(2,1)} %bitcast.10, ...), custom_call_target="tpu_custom_call" | custom-call | tf_op jit(solution)/shard_map/pallas_call | solution.py:271
  10.2 0.7 %collective-permute-done.3.rest_2_ = bf16[4,3328]{1,0:T(4,128)(2,1)S(1)} collective-permute-done((bf16[4,3328]{1,0:T(4,128)(2,1)}, bf16[4,3328]{1,0:T(4,128)(2,1)S(1)}, u32[]{:S(2)}, u32[]{:S(2)}) %collective-permute-start.3) | collective-permute-done | bytes 26656 | tf_op jit(solution)/shard_map/ppermute | solution.py:300
  10.8 0.6 %shard_map.60.refs_0_ = f32[224,128]{1,0:T(8,128)S(1)} custom-call(f32[1,1664]{1,0:T(1,128)S(1)} %get-tuple-element.17.weight, bf16[224,3328]{1,0:T(8,128)(2,1)S(1)} %get-tuple-element.18.rotated, f32[8,1664]{1,0:T(8,128)S(1)} %get-tuple-element.19.cosine, f32[8,1664]{1,0:T(8,128)S(1)} %get-tuple-element.20.sine, f32[224,128]{1,0:T(8,128)S(1)} %get-tuple-element.21.dropped, ...), custom_call_target="tpu_custom_call" | custom-call | tf_op jit(solution)/shard_map/pallas_call | solution.py:271
  11.4 2.5 %collective-permute-start.7 = (f32[224,128]{1,0:T(8,128)S(1)}, f32[224,128]{1,0:T(8,128)S(1)}, u32[]{:S(2)}, u32[]{:S(2)}) collective-permute-start(f32[224,128]{1,0:T(8,128)S(1)} %shard_map.60.refs_0_), channel_id=1, source_target_pairs={{0,24},{8,16},{16,8},{24,0},{1,25},{9,17},{17,9},{25,1},{2,26},{10... | collective-permute-start | bytes 344072 | tf_op jit(solution)/shard_map/ppermute | solution.py:300
  14.0 0.5 %collective-permute-start.6 = (f32[224,128]{1,0:T(8,128)S(1)}, f32[224,128]{1,0:T(8,128)S(1)}, u32[]{:S(2)}, u32[]{:S(2)}) collective-permute-start(f32[224,128]{1,0:T(8,128)S(1)} %shard_map.60.refs_0_), channel_id=1, source_target_pairs={{0,16},{8,24},{16,0},{24,8},{1,17},{9,25},{17,1},{25,9},{2,18},{10... | collective-permute-start | bytes 344072 | tf_op jit(solution)/shard_map/ppermute | solution.py:300
  14.5 0.5 %collective-permute-start.5 = (f32[224,128]{1,0:T(8,128)S(1)}, f32[224,128]{1,0:T(8,128)S(1)}, u32[]{:S(2)}, u32[]{:S(2)}) collective-permute-start(f32[224,128]{1,0:T(8,128)S(1)} %shard_map.60.refs_0_), channel_id=1, source_target_pairs={{0,8},{8,0},{16,24},{24,16},{1,9},{9,1},{17,25},{25,17},{2,10},{10... | collective-permute-start | bytes 344072 | tf_op jit(solution)/shard_map/ppermute | solution.py:300
  15.0 2.5 %collective-permute-done.7.refs_3_ = f32[224,128]{1,0:T(8,128)S(1)} collective-permute-done((f32[224,128]{1,0:T(8,128)S(1)}, f32[224,128]{1,0:T(8,128)S(1)}, u32[]{:S(2)}, u32[]{:S(2)}) %collective-permute-start.7) | collective-permute-done | bytes 114720 | tf_op jit(solution)/shard_map/ppermute | solution.py:300
  17.5 2.1 %collective-permute-done.6.refs_2_ = f32[224,128]{1,0:T(8,128)S(1)} collective-permute-done((f32[224,128]{1,0:T(8,128)S(1)}, f32[224,128]{1,0:T(8,128)S(1)}, u32[]{:S(2)}, u32[]{:S(2)}) %collective-permute-start.6) | collective-permute-done | bytes 114720 | tf_op jit(solution)/shard_map/ppermute | solution.py:300
  19.6 0.1 collective-permute-done.5.refs_1_
  19.7 0.2 shard_map.61
  19.9 0.0 collective-permute-start.8
  20.0 1.2 %collective-permute-done.8.other_stats = f32[32,128]{1,0:T(8,128)S(1)} collective-permute-done((f32[32,128]{1,0:T(8,128)S(1)}, f32[32,128]{1,0:T(8,128)S(1)}, u32[]{:S(2)}, u32[]{:S(2)}) %collective-permute-start.8) | collective-permute-done | bytes 16416 | tf_op jit(solution)/shard_map/ppermute | solution.py:300
  21.1 0.7 %shard_map.62 = (f32[4,3328]{1,0:T(4,128)S(1)}, f32[4,128]{1,0:T(4,128)S(1)}, bf16[4,3456]{1,0:T(4,128)(2,1)S(1)}, bf16[4,3456]{1,0:T(4,128)(2,1)S(1)}, bf16[4,3456]{1,0:T(4,128)(2,1)S(1)}) custom-call(f32[224,128]{1,0:T(8,128)S(1)} %get-tuple-element.23.raised, f32[32,128]{1,0:T(8,128)S(1)} %get-tuple-element.24.own_stats, ...), custom_call_target="tpu_custom_call" | custom-call | tf_op jit(solution)/shard_map/pallas_call | solution.py:271
  21.8 1.3 %collective-permute-start.9 = (bf16[4,3456]{1,0:T(4,128)(2,1)S(1)}, bf16[4,3456]{1,0:T(4,128)(2,1)S(1)}, u32[]{:S(2)}, u32[]{:S(2)}) collective-permute-start(bf16[4,3456]{1,0:T(4,128)(2,1)S(1)} %get-tuple-element.27), channel_id=1, source_target_pairs={{0,2},{1,3},{2,0},{3,1},{4,6},{5,7},{6,4},{7,5},{8,10},{9,11},{10,... | collective-permute-start | bytes 82952 | tf_op jit(solution)/shard_map/ppermute | solution.py:300
  23.1 2.9 %collective-permute-start.10 = (bf16[4,3456]{1,0:T(4,128)(2,1)S(1)}, bf16[4,3456]{1,0:T(4,128)(2,1)S(1)}, u32[]{:S(2)}, u32[]{:S(2)}) collective-permute-start(bf16[4,3456]{1,0:T(4,128)(2,1)S(1)} %get-tuple-element.28), channel_id=1, source_target_pairs={{0,4},{1,5},{2,6},{3,7},{4,0},{5,1},{6,2},{7,3},{8,12},{9,13},{10,... | collective-permute-start | bytes 82952 | tf_op jit(solution)/shard_map/ppermute | solution.py:300
  26.0 0.3 collective-permute-start.11
  26.3 1.6 %collective-permute-done.10.rest_1_ = bf16[4,3456]{1,0:T(4,128)(2,1)S(1)} collective-permute-done((bf16[4,3456]{1,0:T(4,128)(2,1)S(1)}, bf16[4,3456]{1,0:T(4,128)(2,1)S(1)}, u32[]{:S(2)}, u32[]{:S(2)}) %collective-permute-start.10) | collective-permute-done | bytes 27680 | tf_op jit(solution)/shard_map/ppermute | solution.py:300
  27.9 3.8 %collective-permute-done.11.rest_2_ = bf16[4,3456]{1,0:T(4,128)(2,1)S(1)} collective-permute-done((bf16[4,3456]{1,0:T(4,128)(2,1)S(1)}, bf16[4,3456]{1,0:T(4,128)(2,1)S(1)}, u32[]{:S(2)}, u32[]{:S(2)}) %collective-permute-start.11) | collective-permute-done | bytes 27680 | tf_op jit(solution)/shard_map/ppermute | solution.py:300
  31.7 0.7 %shard_map.63 = (f32[4,3328]{1,0:T(4,128)}, f32[1,4]{1,0:T(1,128)}) custom-call(f32[4,3328]{1,0:T(4,128)S(1)} %get-tuple-element.25.own_sums, f32[4,128]{1,0:T(4,128)S(1)} %get-tuple-element.26.own_mass, bf16[4,3456]{1,0:T(4,128)(2,1)S(1)} %collective-permute-done.9.rest_0_, bf16[4,3456]{1,0:T(4,128)(2,1)S(1)} %collective-permute-done.10.rest_1_, ...), custom_call_target="tpu_custom_call" | custom-call | tf_op jit(solution)/shard_map/pallas_call | solution.py:271
  (5 shorter events, 0.0 us)
Async XLA Ops:
  0.6 7.3 %collective-permute-start = (bf16[16,3328]{1,0:T(8,128)(2,1)}, bf16[16,3328]{1,0:T(8,128)(2,1)S(1)}, u32[]{:S(2)}, u32[]{:S(2)}) collective-permute-start(bf16[16,3328]{1,0:T(8,128)(2,1)} %bitcast.5), channel_id=1, source_target_pairs={{0,1},{1,0},{2,3},{3,2},{4,5},{5,4},{6,7},{7,6},{8,9},{9,8},{10,11... | collective-permute-start | bytes 319496 | tf_op jit(solution)/shard_map/ppermute | solution.py:300
  1.2 9.0 %collective-permute-start.4 = (bf16[4,3328]{1,0:T(4,128)(2,1)}, bf16[4,3328]{1,0:T(4,128)(2,1)S(1)}, u32[]{:S(2)}, u32[]{:S(2)}) collective-permute-start(bf16[4,3328]{1,0:T(4,128)(2,1)} %bitcast.7), channel_id=1, source_target_pairs={{0,6},{1,7},{2,4},{3,5},{4,2},{5,3},{6,0},{7,1},{8,14},{9,15},{10,... | collective-permute-start | bytes 79880 | tf_op jit(solution)/shard_map/ppermute | solution.py:300
  5.9 5.0 %collective-permute-start.3 = (bf16[4,3328]{1,0:T(4,128)(2,1)}, bf16[4,3328]{1,0:T(4,128)(2,1)S(1)}, u32[]{:S(2)}, u32[]{:S(2)}) collective-permute-start(bf16[4,3328]{1,0:T(4,128)(2,1)} %bitcast.8), channel_id=1, source_target_pairs={{0,4},{1,5},{2,6},{3,7},{4,0},{5,1},{6,2},{7,3},{8,12},{9,13},{10,... | collective-permute-start | bytes 79880 | tf_op jit(solution)/shard_map/ppermute | solution.py:300
  5.9 5.0 %collective-permute-start.2 = (bf16[4,3328]{1,0:T(4,128)(2,1)}, bf16[4,3328]{1,0:T(4,128)(2,1)S(1)}, u32[]{:S(2)}, u32[]{:S(2)}) collective-permute-start(bf16[4,3328]{1,0:T(4,128)(2,1)} %bitcast.9), channel_id=1, source_target_pairs={{0,2},{1,3},{2,0},{3,1},{4,6},{5,7},{6,4},{7,5},{8,10},{9,11},{10,... | collective-permute-start | bytes 79880 | tf_op jit(solution)/shard_map/ppermute | solution.py:300
  6.5 1.4 %collective-permute-start.1 = (s32[2,8,49]{2,1,0:T(8,128)}, s32[2,8,49]{2,1,0:T(8,128)S(1)}, u32[]{:S(2)}, u32[]{:S(2)}) collective-permute-start(s32[2,8,49]{2,1,0:T(8,128)} %bitcast.11), channel_id=1, source_target_pairs={{0,1},{1,0},{2,3},{3,2},{4,5},{5,4},{6,7},{7,6},{8,9},{9,8},{10,11... | collective-permute-start | bytes 9416 | tf_op jit(solution)/shard_map/ppermute | solution.py:300
  11.4 6.1 %collective-permute-start.7 = (f32[224,128]{1,0:T(8,128)S(1)}, f32[224,128]{1,0:T(8,128)S(1)}, u32[]{:S(2)}, u32[]{:S(2)}) collective-permute-start(f32[224,128]{1,0:T(8,128)S(1)} %shard_map.60.refs_0_), channel_id=1, source_target_pairs={{0,24},{8,16},{16,8},{24,0},{1,25},{9,17},{17,9},{25,1},{2,26},{10... | collective-permute-start | bytes 344072 | tf_op jit(solution)/shard_map/ppermute | solution.py:300
  14.0 5.7 %collective-permute-start.6 = (f32[224,128]{1,0:T(8,128)S(1)}, f32[224,128]{1,0:T(8,128)S(1)}, u32[]{:S(2)}, u32[]{:S(2)}) collective-permute-start(f32[224,128]{1,0:T(8,128)S(1)} %shard_map.60.refs_0_), channel_id=1, source_target_pairs={{0,16},{8,24},{16,0},{24,8},{1,17},{9,25},{17,1},{25,9},{2,18},{10... | collective-permute-start | bytes 344072 | tf_op jit(solution)/shard_map/ppermute | solution.py:300
  14.5 5.3 %collective-permute-start.5 = (f32[224,128]{1,0:T(8,128)S(1)}, f32[224,128]{1,0:T(8,128)S(1)}, u32[]{:S(2)}, u32[]{:S(2)}) collective-permute-start(f32[224,128]{1,0:T(8,128)S(1)} %shard_map.60.refs_0_), channel_id=1, source_target_pairs={{0,8},{8,0},{16,24},{24,16},{1,9},{9,1},{17,25},{25,17},{2,10},{10... | collective-permute-start | bytes 344072 | tf_op jit(solution)/shard_map/ppermute | solution.py:300
  19.9 1.2 %collective-permute-start.8 = (f32[32,128]{1,0:T(8,128)S(1)}, f32[32,128]{1,0:T(8,128)S(1)}, u32[]{:S(2)}, u32[]{:S(2)}) collective-permute-start(f32[32,128]{1,0:T(8,128)S(1)} %get-tuple-element.24.own_stats), channel_id=1, source_target_pairs={{0,1},{1,0},{2,3},{3,2},{4,5},{5,4},{6,7},{7,6},{8,9},{9,8},{10,11... | collective-permute-start | bytes 49160 | tf_op jit(solution)/shard_map/ppermute | solution.py:300
  21.8 4.5 %collective-permute-start.9 = (bf16[4,3456]{1,0:T(4,128)(2,1)S(1)}, bf16[4,3456]{1,0:T(4,128)(2,1)S(1)}, u32[]{:S(2)}, u32[]{:S(2)}) collective-permute-start(bf16[4,3456]{1,0:T(4,128)(2,1)S(1)} %get-tuple-element.27), channel_id=1, source_target_pairs={{0,2},{1,3},{2,0},{3,1},{4,6},{5,7},{6,4},{7,5},{8,10},{9,11},{10,... | collective-permute-start | bytes 82952 | tf_op jit(solution)/shard_map/ppermute | solution.py:300
  23.1 4.8 %collective-permute-start.10 = (bf16[4,3456]{1,0:T(4,128)(2,1)S(1)}, bf16[4,3456]{1,0:T(4,128)(2,1)S(1)}, u32[]{:S(2)}, u32[]{:S(2)}) collective-permute-start(bf16[4,3456]{1,0:T(4,128)(2,1)S(1)} %get-tuple-element.28), channel_id=1, source_target_pairs={{0,4},{1,5},{2,6},{3,7},{4,0},{5,1},{6,2},{7,3},{8,12},{9,13},{10,... | collective-permute-start | bytes 82952 | tf_op jit(solution)/shard_map/ppermute | solution.py:300
  26.0 5.7 %collective-permute-start.11 = (bf16[4,3456]{1,0:T(4,128)(2,1)S(1)}, bf16[4,3456]{1,0:T(4,128)(2,1)S(1)}, u32[]{:S(2)}, u32[]{:S(2)}) collective-permute-start(bf16[4,3456]{1,0:T(4,128)(2,1)S(1)} %get-tuple-element.29), channel_id=1, source_target_pairs={{0,6},{1,7},{2,4},{3,5},{4,2},{5,3},{6,0},{7,1},{8,14},{9,15},{10,... | collective-permute-start | bytes 82952 | tf_op jit(solution)/shard_map/ppermute | solution.py:300
where the time goes:
time: 32.5 us; the launch traced here: 32.4 us
  starting transfers between devices  13.9 us (43%)
  waiting for transfers between devices  13.3 us (41%)
  Pallas kernels  4.48 us (14%)
  between operations  0.68 us (2%)
    ppermute x12, starting transfers between devices, across(): return lax.ppermute(value, axis, [(i, i ^ step) for i in range(size)])  13.9 us
    ppermute x12, waiting for transfers between devices, across(): return lax.ppermute(value, axis, [(i, i ^ step) for i in range(size)])  13.3 us
    pallas_call x5, Pallas kernels, run(): pl.pallas_call(kernel, in_specs=[pl.BlockSpec(memory_space=space) for spa...  4.48 us
  transfers between devices with their start and end apart: 12, of which 8 were waited for; matrix products, arithmetic and copies ran while one was open for 0% of the time, Pallas kernels for 7%

commit v1 on v0

--- a/solution.py
+++ b/solution.py
@@ -21,6 +21,13 @@
 
 def round_up(value, step):
     return -(-value // step) * step
+
+
+def divided(value, by):
+    if by & (by - 1) == 0:
+        return lax.shift_right_logical(value, jnp.int32(by.bit_length() - 1)), value & (by - 1)
+    quotient = jnp.floor((value.astype(F32) + 0.5) * (1.0 / by)).astype(jnp.int32)
+    return quotient, value - quotient * by
 
 
 def dot(a, b, dims):
@@ -44,12 +51,8 @@
     row = lax.broadcasted_iota(jnp.int32, shape, 0)
     index = lax.broadcasted_iota(jnp.int32, shape, 1)
 
-    def modulo(value, period):
-        count = jnp.floor((value.astype(F32) + 0.5) * (1.0 / period)).astype(jnp.int32)
-        return value - count * period
-
-    freq_x = modulo(index * 37 + band * 11, 257) - 128
-    freq_y = modulo(index * 61 + band * 29, 129)
+    freq_x = divided(index * 37 + band * 11, 257)[1] - 128
+    freq_y = divided(index * 61 + band * 29, 129)[1]
     phase = jnp.where(row < half, (row + 1) * freq_x, (row - half + 1) * freq_y)
     phase = jnp.bitwise_and(phase + BOX // 2, BOX - 1) - BOX // 2
     angle = phase.astype(F32) * (2.0 * math.pi / BOX)
@@ -88,24 +91,24 @@
         kept = jnp.concatenate([kept, other_mask[...].reshape(blocks * owners, shifts)], axis=0)
     gone = (1 - kept).astype(F32).astype(BF16)
     rows = kept.shape[0]
-    column = lax.broadcasted_iota(jnp.int32, (shifts, wide), 1)
-    shift = lax.broadcasted_iota(jnp.int32, (shifts, wide), 0)
-    move_y = column // orient
-    column_r = lax.broadcasted_iota(jnp.int32, (rows, wide), 1)
-    row_r = lax.broadcasted_iota(jnp.int32, (rows, wide), 0)
-    slot = (column_r % orient) // owned
+
+    def iota(shape, dim):
+        return lax.broadcasted_iota(jnp.int32, shape, dim)
+
+    step, column = divided(iota((1, side * wide), 1), wide)
+    move_y, place_o = divided(column, orient)
+    slot = divided(place_o, owned)[0]
+    used = move_y < side
+    wanted = jnp.where(used, step * side + move_y, -1)
+    pick = (iota((shifts, side * wide), 0) == wanted).astype(F32).astype(BF16)
     owner = jnp.bitwise_xor(slot, place // pair) * pair + place % pair
-    mine = (row_r % owners == owner) & (column_r < side * orient)
-    per_block = count // blocks
-    spread = (
-        lax.broadcasted_iota(jnp.int32, (total, rows), 0) // per_block
-        == lax.broadcasted_iota(jnp.int32, (total, rows), 1) // owners
-    )
+    mine = divided(iota((rows, 1), 0), owners)[1] == owner
+    spread = divided(iota((total, 1), 0), count // blocks)[0] == divided(iota((1, rows), 1), owners)[0]
     spread = spread.astype(F32).astype(BF16)
+    chosen = jnp.where(mine, dot(gone, pick, ((1,), (0,))), 0.0).astype(BF16)
+    level = PENALTY * dot(spread, chosen, ((1,), (0,)))
     for step in range(side):
-        pick = ((shift == step * side + move_y) & (move_y < side)).astype(F32).astype(BF16)
-        chosen = jnp.where(mine, dot(gone, pick, ((1,), (0,))), 0.0).astype(BF16)
-        dropped[pl.ds(step * total, total), :] = PENALTY * dot(spread, chosen, ((1,), (0,)))
+        dropped[pl.ds(step * total, total), :] = level[:, step * wide : (step + 1) * wide]
     copies[2].wait()
     copies[3].wait()
 
@@ -147,7 +150,7 @@
     norms = jnp.sum(norms, axis=1, keepdims=True)
     column = lax.broadcasted_iota(jnp.int32, (orient, wide), 1)
     row = lax.broadcasted_iota(jnp.int32, (orient, wide), 0)
-    same = (column % orient == row) & (column < side * orient)
+    same = (divided(column, orient)[1] == row) & (column < side * orient)
     level = jnp.sum(jnp.where(same, norms, 0.0), axis=0, keepdims=True)
     cross = dot(rotated[...], turned[...], ((1,), (1,)))
     partial[...] = cross - 0.5 * level - dropped[...]
@@ -208,7 +211,7 @@
     columns = jnp.sum(columns, axis=0, keepdims=True)
     column = lax.broadcasted_iota(jnp.int32, (orient, wide), 1)
     row = lax.broadcasted_iota(jnp.int32, (orient, wide), 0)
-    same = (column % orient == row) & (column < side * orient)
+    same = (divided(column, orient)[1] == row) & (column < side * orient)
     masses = jnp.sum(jnp.where(same, columns, 0.0), axis=1, keepdims=True)
     spread = jnp.broadcast_to(masses, (orient, LANES))
     high = spread.astype(BF16)
@@ -308,6 +311,9 @@
         other, other_masks = images, masks
     for slot in far_first:
         blocks[slot] = across(references, "img", places, slot * pair)
+
+    def far_away(value):
+        return pltpu.with_memory_space_constraint(value, pltpu.MemorySpace.HBM)
 
     def prepare(*refs):
         given, refs = refs[:4], refs[4:]
@@ -329,7 +335,7 @@
             pltpu.SemaphoreType.DMA((4,)),
         ),
         4,
-    )(*[pltpu.with_memory_space_constraint(value, pltpu.MemorySpace.HBM) for value in (images, masks, references, noise_weight)], other, other_masks)
+    )(*[far_away(value) for value in (images, masks, references, noise_weight)], other, other_masks)
 
     partial = call(
         functools.partial(score_kernel, side, slots),

time: 32.5 us -> 31.8 us (0.978)
  Pallas kernels: 4.48 us -> 3.75 us
    pallas_call x5, Pallas kernels: 4.48 us -> 3.75 us  [run(): pl.pallas_call(kernel, in_specs=[pl.BlockSpec(memory_space=space) for spa...]
  transfers between devices with their start and end apart: 12 -> 12, of which waited for: 8 -> 8; matrix products, arithmetic and copies ran while one was open for 0% -> 0% of each run, Pallas kernels for 7% -> 5%
where the time goes in v1:
time: 31.8 us; the launch traced here: 31.6 us
  starting transfers between devices  13.9 us (44%)
  waiting for transfers between devices  13.3 us (42%)
  Pallas kernels  3.75 us (12%)
  between operations  0.68 us (2%)
    ppermute x12, starting transfers between devices, across(): return lax.ppermute(value, axis, [(i, i ^ step) for i in range(size)])  13.9 us
    ppermute x12, waiting for transfers between devices, across(): return lax.ppermute(value, axis, [(i, i ^ step) for i in range(size)])  13.3 us
    pallas_call x5, Pallas kernels, run(): pl.pallas_call(kernel, in_specs=[pl.BlockSpec(memory_space=space) for spa...  3.75 us
  transfers between devices with their start and end apart: 12, of which 8 were waited for; matrix products, arithmetic and copies ran while one was open for 0% of the time, Pallas kernels for 5%

profile of v1, /device:TPU:0, one launch (start us, length us, event | category | flops | bytes accessed | tf_op | source)
XLA Modules:
  0.0 31.6 jit_solution(737247036928833574)
XLA Ops:
  0.6 0.6 %collective-permute-start = (bf16[16,3328]{1,0:T(8,128)(2,1)}, bf16[16,3328]{1,0:T(8,128)(2,1)S(1)}, u32[]{:S(2)}, u32[]{:S(2)}) collective-permute-start(bf16[16,3328]{1,0:T(8,128)(2,1)} %bitcast.5), channel_id=1, source_target_pairs={{0,1},{1,0},{2,3},{3,2},{4,5},{5,4},{6,7},{7,6},{8,9},{9,8},{10,11... | collective-permute-start | bytes 319496 | tf_op jit(solution)/shard_map/ppermute | solution.py:303
  1.2 4.7 %collective-permute-start.4 = (bf16[4,3328]{1,0:T(4,128)(2,1)}, bf16[4,3328]{1,0:T(4,128)(2,1)S(1)}, u32[]{:S(2)}, u32[]{:S(2)}) collective-permute-start(bf16[4,3328]{1,0:T(4,128)(2,1)} %bitcast.7), channel_id=1, source_target_pairs={{0,6},{1,7},{2,4},{3,5},{4,2},{5,3},{6,0},{7,1},{8,14},{9,15},{10,... | collective-permute-start | bytes 79880 | tf_op jit(solution)/shard_map/ppermute | solution.py:303
  5.9 0.0 collective-permute-start.3
  5.9 0.6 %collective-permute-start.2 = (bf16[4,3328]{1,0:T(4,128)(2,1)}, bf16[4,3328]{1,0:T(4,128)(2,1)S(1)}, u32[]{:S(2)}, u32[]{:S(2)}) collective-permute-start(bf16[4,3328]{1,0:T(4,128)(2,1)} %bitcast.9), channel_id=1, source_target_pairs={{0,2},{1,3},{2,0},{3,1},{4,6},{5,7},{6,4},{7,5},{8,10},{9,11},{10,... | collective-permute-start | bytes 79880 | tf_op jit(solution)/shard_map/ppermute | solution.py:303
  6.5 1.4 %collective-permute-done.1.refs_5_ = s32[2,8,49]{2,1,0:T(8,128)S(1)} collective-permute-done((s32[2,8,49]{2,1,0:T(8,128)}, s32[2,8,49]{2,1,0:T(8,128)S(1)}, u32[]{:S(2)}, u32[]{:S(2)}) %collective-permute-start.1) | collective-permute-done | bytes 3168 | tf_op jit(solution)/shard_map/ppermute | solution.py:303
  7.9 1.5 %shard_map.59 = (bf16[224,3328]{1,0:T(8,128)(2,1)S(1)}, f32[8,1664]{1,0:T(8,128)S(1)}, f32[8,1664]{1,0:T(8,128)S(1)}, f32[224,128]{1,0:T(8,128)S(1)}, bf16[4,332...) custom-call(bf16[16,3328]{1,0:T(8,128)(2,1)} %bitcast.6, s32[2,8,49]{2,1,0:T(8,128)} %bitcast.12, bf16[4,3328]{1,0:T(4,128)(2,1)} %bitcast.10, ...), custom_call_target="tpu_custom_call" | custom-call | tf_op jit(solution)/shard_map/pallas_call | solution.py:274
  9.4 1.4 %collective-permute-done.3.rest_2_ = bf16[4,3328]{1,0:T(4,128)(2,1)S(1)} collective-permute-done((bf16[4,3328]{1,0:T(4,128)(2,1)}, bf16[4,3328]{1,0:T(4,128)(2,1)S(1)}, u32[]{:S(2)}, u32[]{:S(2)}) %collective-permute-start.3) | collective-permute-done | bytes 26656 | tf_op jit(solution)/shard_map/ppermute | solution.py:303
  10.8 0.6 %shard_map.60.refs_0_ = f32[224,128]{1,0:T(8,128)S(1)} custom-call(f32[1,1664]{1,0:T(1,128)S(1)} %get-tuple-element.17.weight, bf16[224,3328]{1,0:T(8,128)(2,1)S(1)} %get-tuple-element.18.rotated, f32[8,1664]{1,0:T(8,128)S(1)} %get-tuple-element.19.cosine, f32[8,1664]{1,0:T(8,128)S(1)} %get-tuple-element.20.sine, f32[224,128]{1,0:T(8,128)S(1)} %get-tuple-element.21.dropped, ...), custom_call_target="tpu_custom_call" | custom-call | tf_op jit(solution)/shard_map/pallas_call | solution.py:274
  11.4 2.5 %collective-permute-start.7 = (f32[224,128]{1,0:T(8,128)S(1)}, f32[224,128]{1,0:T(8,128)S(1)}, u32[]{:S(2)}, u32[]{:S(2)}) collective-permute-start(f32[224,128]{1,0:T(8,128)S(1)} %shard_map.60.refs_0_), channel_id=1, source_target_pairs={{0,24},{8,16},{16,8},{24,0},{1,25},{9,17},{17,9},{25,1},{2,26},{10... | collective-permute-start | bytes 344072 | tf_op jit(solution)/shard_map/ppermute | solution.py:303
  14.0 0.5 %collective-permute-start.6 = (f32[224,128]{1,0:T(8,128)S(1)}, f32[224,128]{1,0:T(8,128)S(1)}, u32[]{:S(2)}, u32[]{:S(2)}) collective-permute-start(f32[224,128]{1,0:T(8,128)S(1)} %shard_map.60.refs_0_), channel_id=1, source_target_pairs={{0,16},{8,24},{16,0},{24,8},{1,17},{9,25},{17,1},{25,9},{2,18},{10... | collective-permute-start | bytes 344072 | tf_op jit(solution)/shard_map/ppermute | solution.py:303
  14.5 0.5 %collective-permute-start.5 = (f32[224,128]{1,0:T(8,128)S(1)}, f32[224,128]{1,0:T(8,128)S(1)}, u32[]{:S(2)}, u32[]{:S(2)}) collective-permute-start(f32[224,128]{1,0:T(8,128)S(1)} %shard_map.60.refs_0_), channel_id=1, source_target_pairs={{0,8},{8,0},{16,24},{24,16},{1,9},{9,1},{17,25},{25,17},{2,10},{10... | collective-permute-start | bytes 344072 | tf_op jit(solution)/shard_map/ppermute | solution.py:303
  15.0 2.8 %collective-permute-done.7.refs_3_ = f32[224,128]{1,0:T(8,128)S(1)} collective-permute-done((f32[224,128]{1,0:T(8,128)S(1)}, f32[224,128]{1,0:T(8,128)S(1)}, u32[]{:S(2)}, u32[]{:S(2)}) %collective-permute-start.7) | collective-permute-done | bytes 114720 | tf_op jit(solution)/shard_map/ppermute | solution.py:303
  17.8 1.4 %collective-permute-done.6.refs_2_ = f32[224,128]{1,0:T(8,128)S(1)} collective-permute-done((f32[224,128]{1,0:T(8,128)S(1)}, f32[224,128]{1,0:T(8,128)S(1)}, u32[]{:S(2)}, u32[]{:S(2)}) %collective-permute-start.6) | collective-permute-done | bytes 114720 | tf_op jit(solution)/shard_map/ppermute | solution.py:303
  19.1 0.2 collective-permute-done.5.refs_1_
  19.4 0.2 shard_map.61
  19.6 0.0 collective-permute-start.8
  19.6 1.2 %collective-permute-done.8.other_stats = f32[32,128]{1,0:T(8,128)S(1)} collective-permute-done((f32[32,128]{1,0:T(8,128)S(1)}, f32[32,128]{1,0:T(8,128)S(1)}, u32[]{:S(2)}, u32[]{:S(2)}) %collective-permute-start.8) | collective-permute-done | bytes 16416 | tf_op jit(solution)/shard_map/ppermute | solution.py:303
  20.8 0.7 %shard_map.62 = (f32[4,3328]{1,0:T(4,128)S(1)}, f32[4,128]{1,0:T(4,128)S(1)}, bf16[4,3456]{1,0:T(4,128)(2,1)S(1)}, bf16[4,3456]{1,0:T(4,128)(2,1)S(1)}, bf16[4,3456]{1,0:T(4,128)(2,1)S(1)}) custom-call(f32[224,128]{1,0:T(8,128)S(1)} %get-tuple-element.23.raised, f32[32,128]{1,0:T(8,128)S(1)} %get-tuple-element.24.own_stats, ...), custom_call_target="tpu_custom_call" | custom-call | tf_op jit(solution)/shard_map/pallas_call | solution.py:274
  21.5 0.8 %collective-permute-start.9 = (bf16[4,3456]{1,0:T(4,128)(2,1)S(1)}, bf16[4,3456]{1,0:T(4,128)(2,1)S(1)}, u32[]{:S(2)}, u32[]{:S(2)}) collective-permute-start(bf16[4,3456]{1,0:T(4,128)(2,1)S(1)} %get-tuple-element.27), channel_id=1, source_target_pairs={{0,2},{1,3},{2,0},{3,1},{4,6},{5,7},{6,4},{7,5},{8,10},{9,11},{10,... | collective-permute-start | bytes 82952 | tf_op jit(solution)/shard_map/ppermute | solution.py:303
  22.3 2.9 %collective-permute-start.10 = (bf16[4,3456]{1,0:T(4,128)(2,1)S(1)}, bf16[4,3456]{1,0:T(4,128)(2,1)S(1)}, u32[]{:S(2)}, u32[]{:S(2)}) collective-permute-start(bf16[4,3456]{1,0:T(4,128)(2,1)S(1)} %get-tuple-element.28), channel_id=1, source_target_pairs={{0,4},{1,5},{2,6},{3,7},{4,0},{5,1},{6,2},{7,3},{8,12},{9,13},{10,... | collective-permute-start | bytes 82952 | tf_op jit(solution)/shard_map/ppermute | solution.py:303
  25.3 0.7 %collective-permute-start.11 = (bf16[4,3456]{1,0:T(4,128)(2,1)S(1)}, bf16[4,3456]{1,0:T(4,128)(2,1)S(1)}, u32[]{:S(2)}, u32[]{:S(2)}) collective-permute-start(bf16[4,3456]{1,0:T(4,128)(2,1)S(1)} %get-tuple-element.29), channel_id=1, source_target_pairs={{0,6},{1,7},{2,4},{3,5},{4,2},{5,3},{6,0},{7,1},{8,14},{9,15},{10,... | collective-permute-start | bytes 82952 | tf_op jit(solution)/shard_map/ppermute | solution.py:303
  26.0 1.2 %collective-permute-done.10.rest_1_ = bf16[4,3456]{1,0:T(4,128)(2,1)S(1)} collective-permute-done((bf16[4,3456]{1,0:T(4,128)(2,1)S(1)}, bf16[4,3456]{1,0:T(4,128)(2,1)S(1)}, u32[]{:S(2)}, u32[]{:S(2)}) %collective-permute-start.10) | collective-permute-done | bytes 27680 | tf_op jit(solution)/shard_map/ppermute | solution.py:303
  27.2 3.8 %collective-permute-done.11.rest_2_ = bf16[4,3456]{1,0:T(4,128)(2,1)S(1)} collective-permute-done((bf16[4,3456]{1,0:T(4,128)(2,1)S(1)}, bf16[4,3456]{1,0:T(4,128)(2,1)S(1)}, u32[]{:S(2)}, u32[]{:S(2)}) %collective-permute-start.11) | collective-permute-done | bytes 27680 | tf_op jit(solution)/shard_map/ppermute | solution.py:303
  30.9 0.7 %shard_map.63 = (f32[4,3328]{1,0:T(4,128)}, f32[1,4]{1,0:T(1,128)}) custom-call(f32[4,3328]{1,0:T(4,128)S(1)} %get-tuple-element.25.own_sums, f32[4,128]{1,0:T(4,128)S(1)} %get-tuple-element.26.own_mass, bf16[4,3456]{1,0:T(4,128)(2,1)S(1)} %collective-permute-done.9.rest_0_, bf16[4,3456]{1,0:T(4,128)(2,1)S(1)} %collective-permute-done.10.rest_1_, ...), custom_call_target="tpu_custom_call" | custom-call | tf_op jit(solution)/shard_map/pallas_call | solution.py:274
  (5 shorter events, 0.0 us)
Async XLA Ops:
  0.6 7.3 %collective-permute-start = (bf16[16,3328]{1,0:T(8,128)(2,1)}, bf16[16,3328]{1,0:T(8,128)(2,1)S(1)}, u32[]{:S(2)}, u32[]{:S(2)}) collective-permute-start(bf16[16,3328]{1,0:T(8,128)(2,1)} %bitcast.5), channel_id=1, source_target_pairs={{0,1},{1,0},{2,3},{3,2},{4,5},{5,4},{6,7},{7,6},{8,9},{9,8},{10,11... | collective-permute-start | bytes 319496 | tf_op jit(solution)/shard_map/ppermute | solution.py:303
  1.2 8.2 %collective-permute-start.4 = (bf16[4,3328]{1,0:T(4,128)(2,1)}, bf16[4,3328]{1,0:T(4,128)(2,1)S(1)}, u32[]{:S(2)}, u32[]{:S(2)}) collective-permute-start(bf16[4,3328]{1,0:T(4,128)(2,1)} %bitcast.7), channel_id=1, source_target_pairs={{0,6},{1,7},{2,4},{3,5},{4,2},{5,3},{6,0},{7,1},{8,14},{9,15},{10,... | collective-permute-start | bytes 79880 | tf_op jit(solution)/shard_map/ppermute | solution.py:303
  5.9 5.0 %collective-permute-start.3 = (bf16[4,3328]{1,0:T(4,128)(2,1)}, bf16[4,3328]{1,0:T(4,128)(2,1)S(1)}, u32[]{:S(2)}, u32[]{:S(2)}) collective-permute-start(bf16[4,3328]{1,0:T(4,128)(2,1)} %bitcast.8), channel_id=1, source_target_pairs={{0,4},{1,5},{2,6},{3,7},{4,0},{5,1},{6,2},{7,3},{8,12},{9,13},{10,... | collective-permute-start | bytes 79880 | tf_op jit(solution)/shard_map/ppermute | solution.py:303
  5.9 5.0 %collective-permute-start.2 = (bf16[4,3328]{1,0:T(4,128)(2,1)}, bf16[4,3328]{1,0:T(4,128)(2,1)S(1)}, u32[]{:S(2)}, u32[]{:S(2)}) collective-permute-start(bf16[4,3328]{1,0:T(4,128)(2,1)} %bitcast.9), channel_id=1, source_target_pairs={{0,2},{1,3},{2,0},{3,1},{4,6},{5,7},{6,4},{7,5},{8,10},{9,11},{10,... | collective-permute-start | bytes 79880 | tf_op jit(solution)/shard_map/ppermute | solution.py:303
  6.5 1.4 %collective-permute-start.1 = (s32[2,8,49]{2,1,0:T(8,128)}, s32[2,8,49]{2,1,0:T(8,128)S(1)}, u32[]{:S(2)}, u32[]{:S(2)}) collective-permute-start(s32[2,8,49]{2,1,0:T(8,128)} %bitcast.11), channel_id=1, source_target_pairs={{0,1},{1,0},{2,3},{3,2},{4,5},{5,4},{6,7},{7,6},{8,9},{9,8},{10,11... | collective-permute-start | bytes 9416 | tf_op jit(solution)/shard_map/ppermute | solution.py:303
  11.4 6.3 %collective-permute-start.7 = (f32[224,128]{1,0:T(8,128)S(1)}, f32[224,128]{1,0:T(8,128)S(1)}, u32[]{:S(2)}, u32[]{:S(2)}) collective-permute-start(f32[224,128]{1,0:T(8,128)S(1)} %shard_map.60.refs_0_), channel_id=1, source_target_pairs={{0,24},{8,16},{16,8},{24,0},{1,25},{9,17},{17,9},{25,1},{2,26},{10... | collective-permute-start | bytes 344072 | tf_op jit(solution)/shard_map/ppermute | solution.py:303
  14.0 5.2 %collective-permute-start.6 = (f32[224,128]{1,0:T(8,128)S(1)}, f32[224,128]{1,0:T(8,128)S(1)}, u32[]{:S(2)}, u32[]{:S(2)}) collective-permute-start(f32[224,128]{1,0:T(8,128)S(1)} %shard_map.60.refs_0_), channel_id=1, source_target_pairs={{0,16},{8,24},{16,0},{24,8},{1,17},{9,25},{17,1},{25,9},{2,18},{10... | collective-permute-start | bytes 344072 | tf_op jit(solution)/shard_map/ppermute | solution.py:303
  14.5 4.9 %collective-permute-start.5 = (f32[224,128]{1,0:T(8,128)S(1)}, f32[224,128]{1,0:T(8,128)S(1)}, u32[]{:S(2)}, u32[]{:S(2)}) collective-permute-start(f32[224,128]{1,0:T(8,128)S(1)} %shard_map.60.refs_0_), channel_id=1, source_target_pairs={{0,8},{8,0},{16,24},{24,16},{1,9},{9,1},{17,25},{25,17},{2,10},{10... | collective-permute-start | bytes 344072 | tf_op jit(solution)/shard_map/ppermute | solution.py:303
  19.6 1.2 %collective-permute-start.8 = (f32[32,128]{1,0:T(8,128)S(1)}, f32[32,128]{1,0:T(8,128)S(1)}, u32[]{:S(2)}, u32[]{:S(2)}) collective-permute-start(f32[32,128]{1,0:T(8,128)S(1)} %get-tuple-element.24.own_stats), channel_id=1, source_target_pairs={{0,1},{1,0},{2,3},{3,2},{4,5},{5,4},{6,7},{7,6},{8,9},{9,8},{10,11... | collective-permute-start | bytes 49160 | tf_op jit(solution)/shard_map/ppermute | solution.py:303
  21.5 4.5 %collective-permute-start.9 = (bf16[4,3456]{1,0:T(4,128)(2,1)S(1)}, bf16[4,3456]{1,0:T(4,128)(2,1)S(1)}, u32[]{:S(2)}, u32[]{:S(2)}) collective-permute-start(bf16[4,3456]{1,0:T(4,128)(2,1)S(1)} %get-tuple-element.27), channel_id=1, source_target_pairs={{0,2},{1,3},{2,0},{3,1},{4,6},{5,7},{6,4},{7,5},{8,10},{9,11},{10,... | collective-permute-start | bytes 82952 | tf_op jit(solution)/shard_map/ppermute | solution.py:303
  22.3 4.8 %collective-permute-start.10 = (bf16[4,3456]{1,0:T(4,128)(2,1)S(1)}, bf16[4,3456]{1,0:T(4,128)(2,1)S(1)}, u32[]{:S(2)}, u32[]{:S(2)}) collective-permute-start(bf16[4,3456]{1,0:T(4,128)(2,1)S(1)} %get-tuple-element.28), channel_id=1, source_target_pairs={{0,4},{1,5},{2,6},{3,7},{4,0},{5,1},{6,2},{7,3},{8,12},{9,13},{10,... | collective-permute-start | bytes 82952 | tf_op jit(solution)/shard_map/ppermute | solution.py:303
  25.3 5.7 %collective-permute-start.11 = (bf16[4,3456]{1,0:T(4,128)(2,1)S(1)}, bf16[4,3456]{1,0:T(4,128)(2,1)S(1)}, u32[]{:S(2)}, u32[]{:S(2)}) collective-permute-start(bf16[4,3456]{1,0:T(4,128)(2,1)S(1)} %get-tuple-element.29), channel_id=1, source_target_pairs={{0,6},{1,7},{2,4},{3,5},{4,2},{5,3},{6,0},{7,1},{8,14},{9,15},{10,... | collective-permute-start | bytes 82952 | tf_op jit(solution)/shard_map/ppermute | solution.py:303

commit v2 on v1

--- a/solution.py
+++ b/solution.py
@@ -13,6 +13,8 @@
 PENALTY = 10000.0
 LANES = 128
 NEG = -3.0e38
+TINY = 1.0e-30
+STEPS = 32767.0
 
 
 F32 = jnp.float32
@@ -34,12 +36,11 @@
     return lax.dot_general(a, b, (dims, ((), ())), preferred_element_type=F32)
 
 
-def prepare_kernel(side, pair, slots, axes, given, other, other_mask, results, scratch):
-    rotated, cosine, sine, dropped, own_refs, own_weight = results
+def prepare_kernel(side, pair, slots, owned, axes, given, other, other_mask, results, scratch):
+    rotated, cosine, sine, dropped, own_weight = results
     own, own_mask, sems = scratch
-    owned = own_refs.shape[0]
     copies = []
-    for number, (source, target) in enumerate(zip(given, (own, own_mask, own_refs, own_weight))):
+    for number, (source, target) in enumerate(zip(given, (own, own_mask, own_weight))):
         copies.append(pltpu.make_async_copy(source, target, sems.at[number]))
         copies[-1].start()
     half = side // 2
@@ -59,10 +60,11 @@
     cosine[...] = jnp.cos(angle)
     sine[...] = jnp.sin(angle)
 
-    copies[0].wait()
     count = own.shape[0]
     total = pair * count
-    for part, source in enumerate((own, other)[:pair]):
+    for part, source in reversed(list(enumerate((own, other)[:pair]))):
+        if part == 0:
+            copies[0].wait()
         for start in range(0, coef, LANES):
             lanes, far = pl.ds(start, LANES), pl.ds(coef + start, LANES)
 
@@ -101,59 +103,67 @@
     used = move_y < side
     wanted = jnp.where(used, step * side + move_y, -1)
     pick = (iota((shifts, side * wide), 0) == wanted).astype(F32).astype(BF16)
-    owner = jnp.bitwise_xor(slot, place // pair) * pair + place % pair
+    owner = jnp.bitwise_xor(slot * pair + pair - 1, place)
     mine = divided(iota((rows, 1), 0), owners)[1] == owner
-    spread = divided(iota((total, 1), 0), count // blocks)[0] == divided(iota((1, rows), 1), owners)[0]
+    groups = pair * blocks
+    spread = iota((groups, 1), 0) == divided(iota((1, rows), 1), owners)[0]
     spread = spread.astype(F32).astype(BF16)
     chosen = jnp.where(mine, dot(gone, pick, ((1,), (0,))), 0.0).astype(BF16)
-    level = PENALTY * dot(spread, chosen, ((1,), (0,)))
-    for step in range(side):
-        dropped[pl.ds(step * total, total), :] = level[:, step * wide : (step + 1) * wide]
+    level = dot(spread, chosen, ((1,), (0,)))
+    dropped[...] = jnp.concatenate([level[:, step * wide : (step + 1) * wide] for step in range(side)], axis=0)
     copies[2].wait()
-    copies[3].wait()
-
-
-def score_kernel(side, slots, weight, rotated, cosine, sine, dropped, *rest):
-    blocks, (partial, stacked, turned) = rest[:slots], rest[slots:]
+
+
+def score_kernel(side, weight, rotated, cosine, sine, dropped, *rest):
+    blocks, partial = rest[:-1], rest[-1]
     half = side // 2
     coef = cosine.shape[1]
-    owned = blocks[0].shape[0]
-    orient = slots * owned
-    wide = partial.shape[1]
-    for slot in range(slots):
-        stacked[pl.ds(slot * owned, owned), :] = blocks[slot][...].astype(F32)
-    if wide > side * orient:
-        rest_rows = pl.ds(side * orient, wide - side * orient)
-        turned[rest_rows, :] = jnp.zeros((wide - side * orient, 2 * coef), BF16)
+    orient = len(blocks) * blocks[0].shape[0]
+    rows, wide = rotated.shape[0], partial.shape[1]
     norms = jnp.zeros((orient, LANES), F32)
+    cross = jnp.zeros((rows, wide), F32)
     for start in range(0, coef, LANES):
         lanes, far = pl.ds(start, LANES), pl.ds(coef + start, LANES)
         scale = weight[:, lanes]
-        real, imag = stacked[:, lanes], stacked[:, far]
+        real = jnp.concatenate([block[:, lanes].astype(F32) for block in blocks], axis=0)
+        imag = jnp.concatenate([block[:, far].astype(F32) for block in blocks], axis=0)
         norms = norms + (real * real + imag * imag) * scale
-        real = (real * scale).astype(BF16)
-        imag = (imag * scale).astype(BF16)
-
-        def put(step, a, b):
-            rows = pl.ds((step + half) * orient, orient)
-            turned[rows, lanes] = a.astype(BF16)
-            turned[rows, far] = b.astype(BF16)
-
-        put(0, real, imag)
-        real, imag = real.astype(F32), imag.astype(F32)
+        pieces = {0: ((real * scale).astype(BF16), (imag * scale).astype(BF16))}
+        real, imag = pieces[0][0].astype(F32), pieces[0][1].astype(F32)
         for step in range(1, half + 1):
             c = cosine[half + step - 1 : half + step, lanes]
             s = sine[half + step - 1 : half + step, lanes]
             rc, rs, ic, iss = real * c, real * s, imag * c, imag * s
-            put(step, rc + iss, ic - rs)
-            put(-step, rc - iss, ic + rs)
+            pieces[step] = ((rc + iss).astype(BF16), (ic - rs).astype(BF16))
+            pieces[-step] = ((rc - iss).astype(BF16), (ic + rs).astype(BF16))
+        turned = [jnp.concatenate(pieces[step - half], axis=1) for step in range(side)]
+        if wide > side * orient:
+            turned.append(jnp.zeros((wide - side * orient, 2 * LANES), BF16))
+        turned = jnp.concatenate(turned, axis=0)
+        images = jnp.concatenate([rotated[:, lanes], rotated[:, far]], axis=1)
+        cross = cross + dot(images, turned, ((1,), (1,)))
     norms = jnp.sum(norms, axis=1, keepdims=True)
     column = lax.broadcasted_iota(jnp.int32, (orient, wide), 1)
     row = lax.broadcasted_iota(jnp.int32, (orient, wide), 0)
     same = (divided(column, orient)[1] == row) & (column < side * orient)
     level = jnp.sum(jnp.where(same, norms, 0.0), axis=0, keepdims=True)
-    cross = dot(rotated[...], turned[...], ((1,), (1,)))
-    partial[...] = cross - 0.5 * level - dropped[...]
+    value = cross - 0.5 * level
+    used = side * orient
+    lane = lax.broadcasted_iota(jnp.int32, (rows, wide), 1)
+    largest = jnp.max(jnp.where(lane < used, jnp.abs(value), TINY), axis=1, keepdims=True)
+    exponent = jnp.ceil(jnp.log(largest * (1.0 / STEPS)) * (1.0 / math.log(2.0)))
+    code = jnp.clip(jnp.floor(value / step_size(exponent) + 0.5), -STEPS, STEPS)
+    code = jnp.where(lane < used, code, jnp.where(lane == used, exponent, 0.0))
+    partial[pl.ds(0, rows), :] = code.astype(jnp.int32).astype(jnp.int16)
+    extra = partial.shape[0] - rows
+    flags = dropped[...]
+    if extra > flags.shape[0]:
+        flags = jnp.concatenate([flags, jnp.zeros((extra - flags.shape[0], wide), F32)], axis=0)
+    partial[pl.ds(rows, extra), :] = flags.astype(jnp.int32).astype(jnp.int16)
+
+
+def step_size(exponent):
+    return jnp.exp(exponent * math.log(2.0))
 
 
 def tree_sum(values):
@@ -162,11 +172,18 @@
     return values[0]
 
 
-def raise_kernel(side, used, *refs):
+def raise_kernel(side, used, groups, *refs):
     parts, (raised, stats) = refs[:-2], refs[-2:]
-    score = tree_sum([part[...] for part in parts])
-    rows, wide = score.shape
+    rows, wide = raised.shape
     total = rows // side
+    values, counts = [], []
+    for part in parts:
+        code = part[pl.ds(0, rows), :].astype(jnp.int32).astype(F32)
+        values.append(code * step_size(code[:, used : used + 1]))
+        counts.append(part[pl.ds(rows, part.shape[0] - rows), :].astype(jnp.int32))
+    gone = PENALTY * tree_sum(counts).astype(F32)
+    lines = [jnp.broadcast_to(gone[row : row + 1], (total // groups, wide)) for row in range(side * groups)]
+    score = tree_sum(values) - jnp.concatenate(lines, axis=0)
     lane = lax.broadcasted_iota(jnp.int32, (rows, wide), 1)
     score = jnp.where(lane < used, score, NEG)
     peak = score[:total]
@@ -184,12 +201,12 @@
 
 
 def sum_kernel(side, slots, pair, raised, own_stats, other_stats, rotated, cosine, sine, *rest):
-    own_sums, own_mass, messages, moved = rest[0], rest[1], rest[2 : 1 + slots], rest[1 + slots]
+    near, messages = rest[0], rest[1:]
     half = side // 2
     coef = cosine.shape[1]
     rows, wide = raised.shape
     total = rows // side
-    owned = own_sums.shape[0]
+    owned = near.shape[0]
     orient = slots * owned
     peak, mass = own_stats[:, 0:1], own_stats[:, 1:2]
     if pair > 1:
@@ -218,40 +235,42 @@
     low = (spread - high.astype(F32)).astype(BF16)
     lane = lax.broadcasted_iota(jnp.int32, (orient, LANES), 1)
     tail = jnp.where(lane == 0, high.astype(F32), jnp.where(lane == 1, low.astype(F32), 0.0))
-    own_mass[...] = spread[:owned]
+    near[:, pl.ds(2 * coef, LANES)] = spread[:owned]
     for slot in range(1, slots):
         piece = tail[slot * owned : (slot + 1) * owned]
         messages[slot - 1][:, pl.ds(2 * coef, LANES)] = piece.astype(BF16)
 
-    moved[...] = dot(post, rotated[...], ((0,), (0,)))
+    post = jnp.transpose(post)
     for start in range(0, coef, LANES):
         lanes, far = pl.ds(start, LANES), pl.ds(coef + start, LANES)
 
+        images = jnp.concatenate([rotated[:, lanes], rotated[:, far]], axis=1)
+        moved = dot(post, images, ((1,), (0,)))
+
         def take(step, where):
-            return moved[pl.ds((step + half) * orient, orient), where]
-
-        real, imag = take(0, lanes), take(0, far)
+            return moved[(step + half) * orient : (step + half + 1) * orient, where * LANES : (where + 1) * LANES]
+
+        real, imag = take(0, 0), take(0, 1)
         for step in range(1, half + 1):
             c = cosine[half + step - 1 : half + step, lanes]
             s = sine[half + step - 1 : half + step, lanes]
-            ra, rb = take(step, lanes), take(-step, lanes)
-            ia, ib = take(step, far), take(-step, far)
+            ra, rb = take(step, 0), take(-step, 0)
+            ia, ib = take(step, 1), take(-step, 1)
             real = real + (ra + rb) * c - (ia - ib) * s
             imag = imag + (ia + ib) * c + (ra - rb) * s
-        own_sums[:, lanes] = real[:owned]
-        own_sums[:, far] = imag[:owned]
+        near[:, lanes] = real[:owned]
+        near[:, far] = imag[:owned]
         for slot in range(1, slots):
             part = slice(slot * owned, (slot + 1) * owned)
             messages[slot - 1][:, lanes] = real[part].astype(BF16)
             messages[slot - 1][:, far] = imag[part].astype(BF16)
 
 
-def finish_kernel(own_sums, own_mass, *rest):
+def finish_kernel(near, *rest):
     messages, (sums, mass) = rest[:-2], rest[-2:]
-    wide = sums.shape[1]
-    owned = sums.shape[0]
-    out = own_sums[...]
-    level = own_mass[:, 0:1]
+    owned, wide = sums.shape
+    out = near[:, pl.ds(0, wide)]
+    level = near[:, pl.ds(wide, LANES)][:, 0:1]
     for message in messages:
         out = out + message[:, pl.ds(0, wide)].astype(F32)
         tail = message[:, pl.ds(wide, LANES)].astype(F32)
@@ -297,7 +316,8 @@
     total = count * pair
     orient = slots * owned
     used = side * orient
-    wide = round_up(used, LANES)
+    wide = round_up(used + 1, LANES)
+    groups = pair * masks.shape[0]
 
     def across(value, axis, size, step):
         return lax.ppermute(value, axis, [(i, i ^ step) for i in range(size)])
@@ -307,64 +327,57 @@
     if pair > 1:
         other = across(images, "img", places, 1)
         other_masks = across(masks, "img", places, 1)
+        blocks[0] = across(references, "img", places, 1)
     else:
-        other, other_masks = images, masks
+        other, other_masks, blocks[0] = images, masks, references
     for slot in far_first:
-        blocks[slot] = across(references, "img", places, slot * pair)
+        blocks[slot] = across(references, "img", places, slot * pair + pair - 1)
 
     def far_away(value):
         return pltpu.with_memory_space_constraint(value, pltpu.MemorySpace.HBM)
 
     def prepare(*refs):
-        given, refs = refs[:4], refs[4:]
-        prepare_kernel(side, pair, slots, ("band", "img"), given, refs[0], refs[1], refs[2:8], refs[8:])
-
-    rotated, cosine, sine, dropped, blocks[0], weight = call(
+        given, refs = refs[:3], refs[3:]
+        prepare_kernel(side, pair, slots, owned, ("band", "img"), given, refs[0], refs[1], refs[2:7], refs[7:])
+
+    rotated, cosine, sine, dropped, weight = call(
         prepare,
         (
             shaped((side * total, 2 * coef), BF16),
             shaped((8, coef), F32),
             shaped((8, coef), F32),
-            shaped((side * total, wide), F32),
-            shaped(references.shape, references.dtype),
+            shaped((side * groups, wide), F32),
             shaped(noise_weight.shape, noise_weight.dtype),
         ),
-        (
-            pltpu.VMEM(images.shape, images.dtype),
-            pltpu.VMEM(masks.shape, masks.dtype),
-            pltpu.SemaphoreType.DMA((4,)),
-        ),
-        4,
-    )(*[far_away(value) for value in (images, masks, references, noise_weight)], other, other_masks)
+        (pltpu.VMEM(images.shape, images.dtype), pltpu.VMEM(masks.shape, masks.dtype), pltpu.SemaphoreType.DMA((3,))),
+        3,
+    )(*[far_away(value) for value in (images, masks, noise_weight)], other, other_masks)
 
     partial = call(
-        functools.partial(score_kernel, side, slots),
-        shaped((side * total, wide), F32),
-        (pltpu.VMEM((orient, 2 * coef), F32), pltpu.VMEM((wide, 2 * coef), BF16)),
+        functools.partial(score_kernel, side), shaped((side * total + round_up(side * groups, 16), wide), jnp.int16)
     )(weight, rotated, cosine, sine, dropped, *[blocks[slot] for slot in range(slots)])
 
     parts = {0: partial}
     for step in range(bands - 1, 0, -1):
         parts[step] = across(partial, "band", bands, step)
     raised, stats = call(
-        functools.partial(raise_kernel, side, used),
+        functools.partial(raise_kernel, side, used, groups),
         (shaped((side * total, wide), F32), shaped((total, LANES), F32)),
     )(*[parts[step] for step in range(bands)])
     other_stats = across(stats, "img", places, 1) if pair > 1 else stats
 
-    outs = call(
+    near, *messages = call(
         functools.partial(sum_kernel, side, slots, pair),
-        (shaped((owned, 2 * coef), F32), shaped((owned, LANES), F32))
-        + (shaped((owned, 2 * coef + LANES), BF16),) * (slots - 1),
-        (pltpu.VMEM((wide, 2 * coef), F32),),
+        (shaped((owned, 2 * coef + LANES), F32),) + (shaped((owned, 2 * coef + LANES), BF16),) * (slots - 1),
     )(raised, stats, other_stats, rotated, cosine, sine)
-    own_sums, own_mass, messages = outs[0], outs[1], outs[2:]
     arrived = {}
     for slot in far_first:
-        arrived[slot] = across(messages[slot - 1], "img", places, slot * pair)
+        arrived[slot] = across(messages[slot - 1], "img", places, slot * pair + pair - 1)
+    if pair > 1:
+        near = across(near, "img", places, 1)
     sums, mass = call(
         finish_kernel, (shaped((owned, 2 * coef), F32), shaped((1, owned), F32))
-    )(own_sums, own_mass, *[arrived[slot] for slot in range(1, slots)])
+    )(near, *[arrived[slot] for slot in range(1, slots)])
     return sums[None], mass[0]
 
 

time: 31.8 us -> 28.9 us (0.909)
  waiting for transfers between devices: 13.3 us -> 10.5 us
    ppermute x12 -> x14, waiting for transfers between devices: 13.3 us -> 10.5 us  [across(): return lax.ppermute(value, axis, [(i, i ^ step) for i in range(size)])]
    ppermute x12 -> x14, starting transfers between devices: 13.9 us -> 13.9 us  [across(): return lax.ppermute(value, axis, [(i, i ^ step) for i in range(size)])]
  transfers between devices with their start and end apart: 12 -> 14, of which waited for: 8 -> 7; matrix products, arithmetic and copies ran while one was open for 0% -> 0% of each run, Pallas kernels for 5% -> 5%
where the time goes in v2:
time: 28.9 us; the launch traced here: 28.8 us
  starting transfers between devices  13.9 us (48%)
  waiting for transfers between devices  10.5 us (36%)
  Pallas kernels  3.79 us (13%)
  between operations  0.68 us (2%)
    ppermute x14, starting transfers between devices, across(): return lax.ppermute(value, axis, [(i, i ^ step) for i in range(size)])  13.9 us
    ppermute x14, waiting for transfers between devices, across(): return lax.ppermute(value, axis, [(i, i ^ step) for i in range(size)])  10.5 us
    pallas_call x5, Pallas kernels, run(): pl.pallas_call(kernel, in_specs=[pl.BlockSpec(memory_space=space) for spa...  3.79 us
  transfers between devices with their start and end apart: 14, of which 7 were waited for; matrix products, arithmetic and copies ran while one was open for 0% of the time, Pallas kernels for 5%

profile of v2, /device:TPU:0, one launch (start us, length us, event | category | flops | bytes accessed | tf_op | source)
XLA Modules:
  0.0 28.8 jit_solution(10453889496465833578)
XLA Ops:
  0.6 0.6 %collective-permute-start = (bf16[16,3328]{1,0:T(8,128)(2,1)}, bf16[16,3328]{1,0:T(8,128)(2,1)S(1)}, u32[]{:S(2)}, u32[]{:S(2)}) collective-permute-start(bf16[16,3328]{1,0:T(8,128)(2,1)} %bitcast.5), channel_id=1, source_target_pairs={{0,1},{1,0},{2,3},{3,2},{4,5},{5,4},{6,7},{7,6},{8,9},{9,8},{10,11... | collective-permute-start | bytes 319496 | tf_op jit(solution)/shard_map/ppermute | solution.py:323
  1.2 0.1 collective-permute-start.1
  1.3 4.7 %collective-permute-start.5 = (bf16[4,3328]{1,0:T(4,128)(2,1)}, bf16[4,3328]{1,0:T(4,128)(2,1)S(1)}, u32[]{:S(2)}, u32[]{:S(2)}) collective-permute-start(bf16[4,3328]{1,0:T(4,128)(2,1)} %bitcast.10), channel_id=1, source_target_pairs={{0,7},{1,6},{2,5},{3,4},{4,3},{5,2},{6,1},{7,0},{8,15},{9,14},{10,... | collective-permute-start | bytes 79880 | tf_op jit(solution)/shard_map/ppermute | solution.py:323
  6.0 0.6 %collective-permute-start.3 = (bf16[4,3328]{1,0:T(4,128)(2,1)}, bf16[4,3328]{1,0:T(4,128)(2,1)S(1)}, u32[]{:S(2)}, u32[]{:S(2)}) collective-permute-start(bf16[4,3328]{1,0:T(4,128)(2,1)} %bitcast.12), channel_id=1, source_target_pairs={{0,3},{1,2},{2,1},{3,0},{4,7},{5,6},{6,5},{7,4},{8,11},{9,10},{10,... | collective-permute-start | bytes 79880 | tf_op jit(solution)/shard_map/ppermute | solution.py:323
  6.6 0.1 collective-permute-start.2
  6.7 1.4 %shard_map.59 = (bf16[224,3328]{1,0:T(8,128)(2,1)S(1)}, f32[8,1664]{1,0:T(8,128)S(1)}, f32[8,1664]{1,0:T(8,128)S(1)}, f32[28,128]{1,0:T(8,128)S(1)}, f32[1,1664]{1,0:T(1,128)S(1)}) custom-call(bf16[16,3328]{1,0:T(8,128)(2,1)} %bitcast.6, s32[2,8,49]{2,1,0:T(8,128)} %bitcast.8, f32[1,1664]{1,0:T(1,128)} %refs_2_.1, ...), custom_call_target="tpu_custom_call" | custom-call | tf_op jit(solution)/shard_map/pallas_call | solution.py:293
  8.0 2.3 %collective-permute-done.4.rest_2_ = bf16[4,3328]{1,0:T(4,128)(2,1)S(1)} collective-permute-done((bf16[4,3328]{1,0:T(4,128)(2,1)}, bf16[4,3328]{1,0:T(4,128)(2,1)S(1)}, u32[]{:S(2)}, u32[]{:S(2)}) %collective-permute-start.4) | collective-permute-done | bytes 26656 | tf_op jit(solution)/shard_map/ppermute | solution.py:323
  10.4 0.7 %shard_map.60.refs_0_ = s16[256,128]{1,0:T(8,128)(2,1)S(1)} custom-call(f32[1,1664]{1,0:T(1,128)S(1)} %get-tuple-element.15.weight, bf16[224,3328]{1,0:T(8,128)(2,1)S(1)} %get-tuple-element.16.rotated, f32[8,1664]{1,0:T(8,128)S(1)} %get-tuple-element.17.cosine, f32[8,1664]{1,0:T(8,128)S(1)} %get-tuple-element.18.sine, ...), custom_call_target="tpu_custom_call" | custom-call | tf_op jit(solution)/shard_map/pallas_call | solution.py:293
  11.1 2.5 %collective-permute-start.8 = (s16[256,128]{1,0:T(8,128)(2,1)S(1)}, s16[256,128]{1,0:T(8,128)(2,1)S(1)}, u32[]{:S(2)}, u32[]{:S(2)}) collective-permute-start(s16[256,128]{1,0:T(8,128)(2,1)S(1)} %shard_map.60.refs_0_), channel_id=1, source_target_pairs={{0,24},{8,16},{16,8},{24,0},{1,25},{9,17},{17,9},{25,1},{2,26},{10... | collective-permute-start | bytes 196616 | tf_op jit(solution)/shard_map/ppermute | solution.py:323
  13.6 0.5 %collective-permute-start.7 = (s16[256,128]{1,0:T(8,128)(2,1)S(1)}, s16[256,128]{1,0:T(8,128)(2,1)S(1)}, u32[]{:S(2)}, u32[]{:S(2)}) collective-permute-start(s16[256,128]{1,0:T(8,128)(2,1)S(1)} %shard_map.60.refs_0_), channel_id=1, source_target_pairs={{0,16},{8,24},{16,0},{24,8},{1,17},{9,25},{17,1},{25,9},{2,18},{10... | collective-permute-start | bytes 196616 | tf_op jit(solution)/shard_map/ppermute | solution.py:323
  14.1 0.5 %collective-permute-start.6 = (s16[256,128]{1,0:T(8,128)(2,1)S(1)}, s16[256,128]{1,0:T(8,128)(2,1)S(1)}, u32[]{:S(2)}, u32[]{:S(2)}) collective-permute-start(s16[256,128]{1,0:T(8,128)(2,1)S(1)} %shard_map.60.refs_0_), channel_id=1, source_target_pairs={{0,8},{8,0},{16,24},{24,16},{1,9},{9,1},{17,25},{25,17},{2,10},{10... | collective-permute-start | bytes 196616 | tf_op jit(solution)/shard_map/ppermute | solution.py:323
  14.6 1.9 %collective-permute-done.8.refs_3_ = s16[256,128]{1,0:T(8,128)(2,1)S(1)} collective-permute-done((s16[256,128]{1,0:T(8,128)(2,1)S(1)}, s16[256,128]{1,0:T(8,128)(2,1)S(1)}, u32[]{:S(2)}, u32[]{:S(2)}) %collective-permute-start.8) | collective-permute-done | bytes 65568 | tf_op jit(solution)/shard_map/ppermute | solution.py:323
  16.5 1.4 %collective-permute-done.7.refs_2_ = s16[256,128]{1,0:T(8,128)(2,1)S(1)} collective-permute-done((s16[256,128]{1,0:T(8,128)(2,1)S(1)}, s16[256,128]{1,0:T(8,128)(2,1)S(1)}, u32[]{:S(2)}, u32[]{:S(2)}) %collective-permute-start.7) | collective-permute-done | bytes 65568 | tf_op jit(solution)/shard_map/ppermute | solution.py:323
  17.9 0.5 %collective-permute-done.6.refs_1_ = s16[256,128]{1,0:T(8,128)(2,1)S(1)} collective-permute-done((s16[256,128]{1,0:T(8,128)(2,1)S(1)}, s16[256,128]{1,0:T(8,128)(2,1)S(1)}, u32[]{:S(2)}, u32[]{:S(2)}) %collective-permute-start.6) | collective-permute-done | bytes 65568 | tf_op jit(solution)/shard_map/ppermute | solution.py:323
  18.4 0.4 %shard_map.61 = (f32[224,128]{1,0:T(8,128)S(1)}, f32[32,128]{1,0:T(8,128)S(1)}) custom-call(s16[256,128]{1,0:T(8,128)(2,1)S(1)} %shard_map.60.refs_0_, s16[256,128]{1,0:T(8,128)(2,1)S(1)} %collective-permute-done.6.refs_1_, s16[256,128]{1,0:T(8,128)(2,1)S(1)} %collective-permute-done.7.refs_2_, s16[256,128]{1,0:T(8,128)(2,1)S(1)} %collective-permute-done.8.refs_3_), custom_call_target="tpu_custom_call" | custom-call | tf_op jit(solution)/shard_map/pallas_call | solution.py:293
  18.7 1.2 %collective-permute-done.9.other_stats = f32[32,128]{1,0:T(8,128)S(1)} collective-permute-done((f32[32,128]{1,0:T(8,128)S(1)}, f32[32,128]{1,0:T(8,128)S(1)}, u32[]{:S(2)}, u32[]{:S(2)}) %collective-permute-start.9) | collective-permute-done | bytes 16416 | tf_op jit(solution)/shard_map/ppermute | solution.py:323
  19.9 0.7 %shard_map.62 = (f32[4,3456]{1,0:T(4,128)S(1)}, bf16[4,3456]{1,0:T(4,128)(2,1)S(1)}, bf16[4,3456]{1,0:T(4,128)(2,1)S(1)}, bf16[4,3456]{1,0:T(4,128)(2,1)S(1)}) custom-call(f32[224,128]{1,0:T(8,128)S(1)} %get-tuple-element.20.raised, f32[32,128]{1,0:T(8,128)S(1)} %get-tuple-element.21.own_stats, f32[32,128]{1,0:T(8,128)S(1)} %collective-permute-done.9.other_stats, ...), custom_call_target="tpu_custom_call" | custom-call | tf_op jit(solution)/shard_map/pallas_call | solution.py:293
  20.6 0.2 collective-permute-start.10
  20.8 0.5 %collective-permute-start.11 = (bf16[4,3456]{1,0:T(4,128)(2,1)S(1)}, bf16[4,3456]{1,0:T(4,128)(2,1)S(1)}, u32[]{:S(2)}, u32[]{:S(2)}) collective-permute-start(bf16[4,3456]{1,0:T(4,128)(2,1)S(1)} %get-tuple-element.23), channel_id=1, source_target_pairs={{0,3},{1,2},{2,1},{3,0},{4,7},{5,6},{6,5},{7,4},{8,11},{9,10},{10,... | collective-permute-start | bytes 82952 | tf_op jit(solution)/shard_map/ppermute | solution.py:323
  21.3 1.6 %collective-permute-start.12 = (bf16[4,3456]{1,0:T(4,128)(2,1)S(1)}, bf16[4,3456]{1,0:T(4,128)(2,1)S(1)}, u32[]{:S(2)}, u32[]{:S(2)}) collective-permute-start(bf16[4,3456]{1,0:T(4,128)(2,1)S(1)} %get-tuple-element.24), channel_id=1, source_target_pairs={{0,5},{1,4},{2,7},{3,6},{4,1},{5,0},{6,3},{7,2},{8,13},{9,12},{10,... | collective-permute-start | bytes 82952 | tf_op jit(solution)/shard_map/ppermute | solution.py:323
  22.9 2.0 %collective-permute-start.13 = (bf16[4,3456]{1,0:T(4,128)(2,1)S(1)}, bf16[4,3456]{1,0:T(4,128)(2,1)S(1)}, u32[]{:S(2)}, u32[]{:S(2)}) collective-permute-start(bf16[4,3456]{1,0:T(4,128)(2,1)S(1)} %get-tuple-element.25), channel_id=1, source_target_pairs={{0,7},{1,6},{2,5},{3,4},{4,3},{5,2},{6,1},{7,0},{8,15},{9,14},{10,... | collective-permute-start | bytes 82952 | tf_op jit(solution)/shard_map/ppermute | solution.py:323
  24.9 0.7 %collective-permute-done.12.rest_1_ = bf16[4,3456]{1,0:T(4,128)(2,1)S(1)} collective-permute-done((bf16[4,3456]{1,0:T(4,128)(2,1)S(1)}, bf16[4,3456]{1,0:T(4,128)(2,1)S(1)}, u32[]{:S(2)}, u32[]{:S(2)}) %collective-permute-start.12) | collective-permute-done | bytes 27680 | tf_op jit(solution)/shard_map/ppermute | solution.py:323
  25.5 2.6 %collective-permute-done.13.rest_2_ = bf16[4,3456]{1,0:T(4,128)(2,1)S(1)} collective-permute-done((bf16[4,3456]{1,0:T(4,128)(2,1)S(1)}, bf16[4,3456]{1,0:T(4,128)(2,1)S(1)}, u32[]{:S(2)}, u32[]{:S(2)}) %collective-permute-start.13) | collective-permute-done | bytes 27680 | tf_op jit(solution)/shard_map/ppermute | solution.py:323
  28.1 0.7 %shard_map.63 = (f32[4,3328]{1,0:T(4,128)}, f32[1,4]{1,0:T(1,128)}) custom-call(f32[4,3456]{1,0:T(4,128)S(1)} %collective-permute-done.10.near, bf16[4,3456]{1,0:T(4,128)(2,1)S(1)} %collective-permute-done.11.rest_0_, bf16[4,3456]{1,0:T(4,128)(2,1)S(1)} %collective-permute-done.12.rest_1_, bf16[4,3456]{1,0:T(4,128)(2,1)S(1)} %collective-permute-done.13.rest_2_), custom_call_target="tpu_custom_call" | custom-call | tf_op jit(solution)/shard_map/pallas_call | solution.py:293
  (9 shorter events, 0.0 us)
Async XLA Ops:
  0.6 6.0 %collective-permute-start = (bf16[16,3328]{1,0:T(8,128)(2,1)}, bf16[16,3328]{1,0:T(8,128)(2,1)S(1)}, u32[]{:S(2)}, u32[]{:S(2)}) collective-permute-start(bf16[16,3328]{1,0:T(8,128)(2,1)} %bitcast.5), channel_id=1, source_target_pairs={{0,1},{1,0},{2,3},{3,2},{4,5},{5,4},{6,7},{7,6},{8,9},{9,8},{10,11... | collective-permute-start | bytes 319496 | tf_op jit(solution)/shard_map/ppermute | solution.py:323
  1.2 5.4 %collective-permute-start.1 = (s32[2,8,49]{2,1,0:T(8,128)}, s32[2,8,49]{2,1,0:T(8,128)S(1)}, u32[]{:S(2)}, u32[]{:S(2)}) collective-permute-start(s32[2,8,49]{2,1,0:T(8,128)} %bitcast.7), channel_id=1, source_target_pairs={{0,1},{1,0},{2,3},{3,2},{4,5},{5,4},{6,7},{7,6},{8,9},{9,8},{10,11... | collective-permute-start | bytes 9416 | tf_op jit(solution)/shard_map/ppermute | solution.py:323
  1.3 6.8 %collective-permute-start.5 = (bf16[4,3328]{1,0:T(4,128)(2,1)}, bf16[4,3328]{1,0:T(4,128)(2,1)S(1)}, u32[]{:S(2)}, u32[]{:S(2)}) collective-permute-start(bf16[4,3328]{1,0:T(4,128)(2,1)} %bitcast.10), channel_id=1, source_target_pairs={{0,7},{1,6},{2,5},{3,4},{4,3},{5,2},{6,1},{7,0},{8,15},{9,14},{10,... | collective-permute-start | bytes 79880 | tf_op jit(solution)/shard_map/ppermute | solution.py:323
  6.0 4.4 %collective-permute-start.4 = (bf16[4,3328]{1,0:T(4,128)(2,1)}, bf16[4,3328]{1,0:T(4,128)(2,1)S(1)}, u32[]{:S(2)}, u32[]{:S(2)}) collective-permute-start(bf16[4,3328]{1,0:T(4,128)(2,1)} %bitcast.11), channel_id=1, source_target_pairs={{0,5},{1,4},{2,7},{3,6},{4,1},{5,0},{6,3},{7,2},{8,13},{9,12},{10,... | collective-permute-start | bytes 79880 | tf_op jit(solution)/shard_map/ppermute | solution.py:323
  6.0 4.4 %collective-permute-start.3 = (bf16[4,3328]{1,0:T(4,128)(2,1)}, bf16[4,3328]{1,0:T(4,128)(2,1)S(1)}, u32[]{:S(2)}, u32[]{:S(2)}) collective-permute-start(bf16[4,3328]{1,0:T(4,128)(2,1)} %bitcast.12), channel_id=1, source_target_pairs={{0,3},{1,2},{2,1},{3,0},{4,7},{5,6},{6,5},{7,4},{8,11},{9,10},{10,... | collective-permute-start | bytes 79880 | tf_op jit(solution)/shard_map/ppermute | solution.py:323
  6.6 3.8 %collective-permute-start.2 = (bf16[4,3328]{1,0:T(4,128)(2,1)}, bf16[4,3328]{1,0:T(4,128)(2,1)S(1)}, u32[]{:S(2)}, u32[]{:S(2)}) collective-permute-start(bf16[4,3328]{1,0:T(4,128)(2,1)} %bitcast.13), channel_id=1, source_target_pairs={{0,1},{1,0},{2,3},{3,2},{4,5},{5,4},{6,7},{7,6},{8,9},{9,8},{10,11... | collective-permute-start | bytes 79880 | tf_op jit(solution)/shard_map/ppermute | solution.py:323
  11.1 5.4 %collective-permute-start.8 = (s16[256,128]{1,0:T(8,128)(2,1)S(1)}, s16[256,128]{1,0:T(8,128)(2,1)S(1)}, u32[]{:S(2)}, u32[]{:S(2)}) collective-permute-start(s16[256,128]{1,0:T(8,128)(2,1)S(1)} %shard_map.60.refs_0_), channel_id=1, source_target_pairs={{0,24},{8,16},{16,8},{24,0},{1,25},{9,17},{17,9},{25,1},{2,26},{10... | collective-permute-start | bytes 196616 | tf_op jit(solution)/shard_map/ppermute | solution.py:323
  13.6 4.3 %collective-permute-start.7 = (s16[256,128]{1,0:T(8,128)(2,1)S(1)}, s16[256,128]{1,0:T(8,128)(2,1)S(1)}, u32[]{:S(2)}, u32[]{:S(2)}) collective-permute-start(s16[256,128]{1,0:T(8,128)(2,1)S(1)} %shard_map.60.refs_0_), channel_id=1, source_target_pairs={{0,16},{8,24},{16,0},{24,8},{1,17},{9,25},{17,1},{25,9},{2,18},{10... | collective-permute-start | bytes 196616 | tf_op jit(solution)/shard_map/ppermute | solution.py:323
  14.1 4.3 %collective-permute-start.6 = (s16[256,128]{1,0:T(8,128)(2,1)S(1)}, s16[256,128]{1,0:T(8,128)(2,1)S(1)}, u32[]{:S(2)}, u32[]{:S(2)}) collective-permute-start(s16[256,128]{1,0:T(8,128)(2,1)S(1)} %shard_map.60.refs_0_), channel_id=1, source_target_pairs={{0,8},{8,0},{16,24},{24,16},{1,9},{9,1},{17,25},{25,17},{2,10},{10... | collective-permute-start | bytes 196616 | tf_op jit(solution)/shard_map/ppermute | solution.py:323
  18.7 1.2 %collective-permute-start.9 = (f32[32,128]{1,0:T(8,128)S(1)}, f32[32,128]{1,0:T(8,128)S(1)}, u32[]{:S(2)}, u32[]{:S(2)}) collective-permute-start(f32[32,128]{1,0:T(8,128)S(1)} %get-tuple-element.21.own_stats), channel_id=1, source_target_pairs={{0,1},{1,0},{2,3},{3,2},{4,5},{5,4},{6,7},{7,6},{8,9},{9,8},{10,11... | collective-permute-start | bytes 49160 | tf_op jit(solution)/shard_map/ppermute | solution.py:323
  20.6 7.5 %collective-permute-start.10 = (f32[4,3456]{1,0:T(4,128)S(1)}, f32[4,3456]{1,0:T(4,128)S(1)}, u32[]{:S(2)}, u32[]{:S(2)}) collective-permute-start(f32[4,3456]{1,0:T(4,128)S(1)} %get-tuple-element.22), channel_id=1, source_target_pairs={{0,1},{1,0},{2,3},{3,2},{4,5},{5,4},{6,7},{7,6},{8,9},{9,8},{10,11... | collective-permute-start | bytes 165896 | tf_op jit(solution)/shard_map/ppermute | solution.py:323
  20.8 4.1 %collective-permute-start.11 = (bf16[4,3456]{1,0:T(4,128)(2,1)S(1)}, bf16[4,3456]{1,0:T(4,128)(2,1)S(1)}, u32[]{:S(2)}, u32[]{:S(2)}) collective-permute-start(bf16[4,3456]{1,0:T(4,128)(2,1)S(1)} %get-tuple-element.23), channel_id=1, source_target_pairs={{0,3},{1,2},{2,1},{3,0},{4,7},{5,6},{6,5},{7,4},{8,11},{9,10},{10,... | collective-permute-start | bytes 82952 | tf_op jit(solution)/shard_map/ppermute | solution.py:323
  21.3 4.2 %collective-permute-start.12 = (bf16[4,3456]{1,0:T(4,128)(2,1)S(1)}, bf16[4,3456]{1,0:T(4,128)(2,1)S(1)}, u32[]{:S(2)}, u32[]{:S(2)}) collective-permute-start(bf16[4,3456]{1,0:T(4,128)(2,1)S(1)} %get-tuple-element.24), channel_id=1, source_target_pairs={{0,5},{1,4},{2,7},{3,6},{4,1},{5,0},{6,3},{7,2},{8,13},{9,12},{10,... | collective-permute-start | bytes 82952 | tf_op jit(solution)/shard_map/ppermute | solution.py:323
  22.9 5.2 %collective-permute-start.13 = (bf16[4,3456]{1,0:T(4,128)(2,1)S(1)}, bf16[4,3456]{1,0:T(4,128)(2,1)S(1)}, u32[]{:S(2)}, u32[]{:S(2)}) collective-permute-start(bf16[4,3456]{1,0:T(4,128)(2,1)S(1)} %get-tuple-element.25), channel_id=1, source_target_pairs={{0,7},{1,6},{2,5},{3,4},{4,3},{5,2},{6,1},{7,0},{8,15},{9,14},{10,... | collective-permute-start | bytes 82952 | tf_op jit(solution)/shard_map/ppermute | solution.py:323

commit v3 on v2

--- a/solution.py
+++ b/solution.py
@@ -168,22 +168,32 @@
 
 def tree_sum(values):
     while len(values) > 1:
-        values = [a + b for a, b in zip(values[0::2], values[1::2])]
+        left = values[len(values) // 2 * 2 :]
+        values = [a + b for a, b in zip(values[0::2], values[1::2])] + left
     return values[0]
 
 
-def raise_kernel(side, used, groups, *refs):
-    parts, (raised, stats) = refs[:-2], refs[-2:]
+def decode(part, rows, used):
+    code = part[pl.ds(0, rows), :].astype(jnp.int32).astype(F32)
+    value = code * step_size(code[:, used : used + 1])
+    return value, part[pl.ds(rows, part.shape[0] - rows), :].astype(jnp.int32)
+
+
+def decode_kernel(used, *refs):
+    parts, (first, rest, counts) = refs[:-3], refs[-3:]
+    decoded = [decode(part, first.shape[0], used) for part in parts]
+    first[...] = decoded[0][0]
+    rest[...] = tree_sum([value for value, _ in decoded[1:]])
+    counts[...] = sum(count for _, count in decoded)
+
+
+def raise_kernel(side, used, groups, last, first, rest, early, raised, stats):
     rows, wide = raised.shape
     total = rows // side
-    values, counts = [], []
-    for part in parts:
-        code = part[pl.ds(0, rows), :].astype(jnp.int32).astype(F32)
-        values.append(code * step_size(code[:, used : used + 1]))
-        counts.append(part[pl.ds(rows, part.shape[0] - rows), :].astype(jnp.int32))
-    gone = PENALTY * tree_sum(counts).astype(F32)
+    value, count = decode(last, rows, used)
+    gone = PENALTY * (early[...] + count).astype(F32)
     lines = [jnp.broadcast_to(gone[row : row + 1], (total // groups, wide)) for row in range(side * groups)]
-    score = tree_sum(values) - jnp.concatenate(lines, axis=0)
+    score = ((first[...] + value) + rest[...]) - jnp.concatenate(lines, axis=0)
     lane = lax.broadcasted_iota(jnp.int32, (rows, wide), 1)
     score = jnp.where(lane < used, score, NEG)
     peak = score[:total]
@@ -360,10 +370,14 @@
     parts = {0: partial}
     for step in range(bands - 1, 0, -1):
         parts[step] = across(partial, "band", bands, step)
+    plane = shaped((side * total, wide), F32)
+    flags = partial.shape[0] - side * total
+    early = call(
+        functools.partial(decode_kernel, used), (plane, plane, shaped((flags, wide), jnp.int32))
+    )(*[parts[step] for step in range(bands) if step != 1])
     raised, stats = call(
-        functools.partial(raise_kernel, side, used, groups),
-        (shaped((side * total, wide), F32), shaped((total, LANES), F32)),
-    )(*[parts[step] for step in range(bands)])
+        functools.partial(raise_kernel, side, used, groups), (plane, shaped((total, LANES), F32))
+    )(parts[1], *early)
     other_stats = across(stats, "img", places, 1) if pair > 1 else stats
 
     near, *messages = call(

time: 28.9 us -> 29.8 us (1.031)
  starting transfers between devices: 13.9 us -> 14.5 us
    ppermute x14, starting transfers between devices: 13.9 us -> 14.5 us  [across(): return lax.ppermute(value, axis, [(i, i ^ step) for i in range(size)])]
    pallas_call x5 -> x6, Pallas kernels: 3.79 us -> 3.86 us  [run(): pl.pallas_call(kernel, in_specs=[pl.BlockSpec(memory_space=space) for spa...]
  transfers between devices with their start and end apart: 14 -> 14, of which waited for: 7 -> 8; matrix products, arithmetic and copies ran while one was open for 0% -> 0% of each run, Pallas kernels for 5% -> 5%
where the time goes in v3:
time: 29.8 us; the launch traced here: 29.7 us
  starting transfers between devices  14.5 us (49%)
  waiting for transfers between devices  10.6 us (36%)
  Pallas kernels  3.86 us (13%)
  between operations  0.7 us (2%)
    ppermute x14, starting transfers between devices, across(): return lax.ppermute(value, axis, [(i, i ^ step) for i in range(size)])  14.5 us
    ppermute x14, waiting for transfers between devices, across(): return lax.ppermute(value, axis, [(i, i ^ step) for i in range(size)])  10.6 us
    pallas_call x6, Pallas kernels, run(): pl.pallas_call(kernel, in_specs=[pl.BlockSpec(memory_space=space) for spa...  3.86 us
  transfers between devices with their start and end apart: 14, of which 8 were waited for; matrix products, arithmetic and copies ran while one was open for 0% of the time, Pallas kernels for 5%

profile of v3, /device:TPU:0, one launch (start us, length us, event | category | flops | bytes accessed | tf_op | source)
XLA Modules:
  0.0 29.7 jit_solution(6758239549868859376)
XLA Ops:
  0.6 0.6 %collective-permute-start = (bf16[16,3328]{1,0:T(8,128)(2,1)}, bf16[16,3328]{1,0:T(8,128)(2,1)S(1)}, u32[]{:S(2)}, u32[]{:S(2)}) collective-permute-start(bf16[16,3328]{1,0:T(8,128)(2,1)} %bitcast.5), channel_id=1, source_target_pairs={{0,1},{1,0},{2,3},{3,2},{4,5},{5,4},{6,7},{7,6},{8,9},{9,8},{10,11... | collective-permute-start | bytes 319496 | tf_op jit(solution)/shard_map/ppermute | solution.py:333
  1.3 0.4 %collective-permute-start.2 = (bf16[4,3328]{1,0:T(4,128)(2,1)}, bf16[4,3328]{1,0:T(4,128)(2,1)S(1)}, u32[]{:S(2)}, u32[]{:S(2)}) collective-permute-start(bf16[4,3328]{1,0:T(4,128)(2,1)} %bitcast.10), channel_id=1, source_target_pairs={{0,1},{1,0},{2,3},{3,2},{4,5},{5,4},{6,7},{7,6},{8,9},{9,8},{10,11... | collective-permute-start | bytes 79880 | tf_op jit(solution)/shard_map/ppermute | solution.py:333
  1.7 2.7 %collective-permute-start.3 = (bf16[4,3328]{1,0:T(4,128)(2,1)}, bf16[4,3328]{1,0:T(4,128)(2,1)S(1)}, u32[]{:S(2)}, u32[]{:S(2)}) collective-permute-start(bf16[4,3328]{1,0:T(4,128)(2,1)} %bitcast.11), channel_id=1, source_target_pairs={{0,3},{1,2},{2,1},{3,0},{4,7},{5,6},{6,5},{7,4},{8,11},{9,10},{10,... | collective-permute-start | bytes 79880 | tf_op jit(solution)/shard_map/ppermute | solution.py:333
  4.4 2.3 %collective-permute-start.4 = (bf16[4,3328]{1,0:T(4,128)(2,1)}, bf16[4,3328]{1,0:T(4,128)(2,1)S(1)}, u32[]{:S(2)}, u32[]{:S(2)}) collective-permute-start(bf16[4,3328]{1,0:T(4,128)(2,1)} %bitcast.12), channel_id=1, source_target_pairs={{0,5},{1,4},{2,7},{3,6},{4,1},{5,0},{6,3},{7,2},{8,13},{9,12},{10,... | collective-permute-start | bytes 79880 | tf_op jit(solution)/shard_map/ppermute | solution.py:333
  6.7 0.6 %collective-permute-start.5 = (bf16[4,3328]{1,0:T(4,128)(2,1)}, bf16[4,3328]{1,0:T(4,128)(2,1)S(1)}, u32[]{:S(2)}, u32[]{:S(2)}) collective-permute-start(bf16[4,3328]{1,0:T(4,128)(2,1)} %bitcast.13), channel_id=1, source_target_pairs={{0,7},{1,6},{2,5},{3,4},{4,3},{5,2},{6,1},{7,0},{8,15},{9,14},{10,... | collective-permute-start | bytes 79880 | tf_op jit(solution)/shard_map/ppermute | solution.py:333
  7.3 1.4 %shard_map.59 = (bf16[224,3328]{1,0:T(8,128)(2,1)S(1)}, f32[8,1664]{1,0:T(8,128)S(1)}, f32[8,1664]{1,0:T(8,128)S(1)}, f32[28,128]{1,0:T(8,128)S(1)}, f32[1,1664]{1,0:T(1,128)S(1)}) custom-call(bf16[16,3328]{1,0:T(8,128)(2,1)} %bitcast.6, s32[2,8,49]{2,1,0:T(8,128)} %bitcast.8, f32[1,1664]{1,0:T(1,128)} %refs_2_.1, ...), custom_call_target="tpu_custom_call" | custom-call | tf_op jit(solution)/shard_map/pallas_call | solution.py:303
  8.7 0.6 %collective-permute-done.4.rest_2_ = bf16[4,3328]{1,0:T(4,128)(2,1)S(1)} collective-permute-done((bf16[4,3328]{1,0:T(4,128)(2,1)}, bf16[4,3328]{1,0:T(4,128)(2,1)S(1)}, u32[]{:S(2)}, u32[]{:S(2)}) %collective-permute-start.4) | collective-permute-done | bytes 26656 | tf_op jit(solution)/shard_map/ppermute | solution.py:333
  9.2 2.7 %collective-permute-done.5.rest_3_ = bf16[4,3328]{1,0:T(4,128)(2,1)S(1)} collective-permute-done((bf16[4,3328]{1,0:T(4,128)(2,1)}, bf16[4,3328]{1,0:T(4,128)(2,1)S(1)}, u32[]{:S(2)}, u32[]{:S(2)}) %collective-permute-start.5) | collective-permute-done | bytes 26656 | tf_op jit(solution)/shard_map/ppermute | solution.py:333
  11.9 0.7 %shard_map.60.refs_0_ = s16[256,128]{1,0:T(8,128)(2,1)S(1)} custom-call(f32[1,1664]{1,0:T(1,128)S(1)} %get-tuple-element.18.weight, bf16[224,3328]{1,0:T(8,128)(2,1)S(1)} %get-tuple-element.19.rotated, f32[8,1664]{1,0:T(8,128)S(1)} %get-tuple-element.20.cosine, f32[8,1664]{1,0:T(8,128)S(1)} %get-tuple-element.21.sine, ...), custom_call_target="tpu_custom_call" | custom-call | tf_op jit(solution)/shard_map/pallas_call | solution.py:303
  12.6 1.6 %collective-permute-start.7 = (s16[256,128]{1,0:T(8,128)(2,1)S(1)}, s16[256,128]{1,0:T(8,128)(2,1)S(1)}, u32[]{:S(2)}, u32[]{:S(2)}) collective-permute-start(s16[256,128]{1,0:T(8,128)(2,1)S(1)} %shard_map.60.refs_0_), channel_id=1, source_target_pairs={{0,16},{8,24},{16,0},{24,8},{1,17},{9,25},{17,1},{25,9},{2,18},{10... | collective-permute-start | bytes 196616 | tf_op jit(solution)/shard_map/ppermute | solution.py:333
  14.2 1.4 %collective-permute-start.8 = (s16[256,128]{1,0:T(8,128)(2,1)S(1)}, s16[256,128]{1,0:T(8,128)(2,1)S(1)}, u32[]{:S(2)}, u32[]{:S(2)}) collective-permute-start(s16[256,128]{1,0:T(8,128)(2,1)S(1)} %shard_map.60.refs_0_), channel_id=1, source_target_pairs={{0,24},{8,16},{16,8},{24,0},{1,25},{9,17},{17,9},{25,1},{2,26},{10... | collective-permute-start | bytes 196616 | tf_op jit(solution)/shard_map/ppermute | solution.py:333
  15.7 0.5 %collective-permute-start.6 = (s16[256,128]{1,0:T(8,128)(2,1)S(1)}, s16[256,128]{1,0:T(8,128)(2,1)S(1)}, u32[]{:S(2)}, u32[]{:S(2)}) collective-permute-start(s16[256,128]{1,0:T(8,128)(2,1)S(1)} %shard_map.60.refs_0_), channel_id=1, source_target_pairs={{0,8},{8,0},{16,24},{24,16},{1,9},{9,1},{17,25},{25,17},{2,10},{10... | collective-permute-start | bytes 196616 | tf_op jit(solution)/shard_map/ppermute | solution.py:333
  16.2 0.9 %collective-permute-done.7.refs_1_ = s16[256,128]{1,0:T(8,128)(2,1)S(1)} collective-permute-done((s16[256,128]{1,0:T(8,128)(2,1)S(1)}, s16[256,128]{1,0:T(8,128)(2,1)S(1)}, u32[]{:S(2)}, u32[]{:S(2)}) %collective-permute-start.7) | collective-permute-done | bytes 65568 | tf_op jit(solution)/shard_map/ppermute | solution.py:333
  17.1 2.6 %collective-permute-done.8.refs_2_ = s16[256,128]{1,0:T(8,128)(2,1)S(1)} collective-permute-done((s16[256,128]{1,0:T(8,128)(2,1)S(1)}, s16[256,128]{1,0:T(8,128)(2,1)S(1)}, u32[]{:S(2)}, u32[]{:S(2)}) %collective-permute-start.8) | collective-permute-done | bytes 65568 | tf_op jit(solution)/shard_map/ppermute | solution.py:333
  19.7 0.2 shard_map.61
  19.9 0.3 shard_map.62
  20.3 1.2 %collective-permute-done.9.other_stats = f32[32,128]{1,0:T(8,128)S(1)} collective-permute-done((f32[32,128]{1,0:T(8,128)S(1)}, f32[32,128]{1,0:T(8,128)S(1)}, u32[]{:S(2)}, u32[]{:S(2)}) %collective-permute-start.9) | collective-permute-done | bytes 16416 | tf_op jit(solution)/shard_map/ppermute | solution.py:333
  21.4 0.7 %shard_map.63 = (f32[4,3456]{1,0:T(4,128)S(1)}, bf16[4,3456]{1,0:T(4,128)(2,1)S(1)}, bf16[4,3456]{1,0:T(4,128)(2,1)S(1)}, bf16[4,3456]{1,0:T(4,128)(2,1)S(1)}) custom-call(f32[224,128]{1,0:T(8,128)S(1)} %get-tuple-element.26.raised, f32[32,128]{1,0:T(8,128)S(1)} %get-tuple-element.27.own_stats, f32[32,128]{1,0:T(8,128)S(1)} %collective-permute-done.9.other_stats, ...), custom_call_target="tpu_custom_call" | custom-call | tf_op jit(solution)/shard_map/pallas_call | solution.py:303
  22.1 0.2 collective-permute-start.10
  22.3 1.6 %collective-permute-start.12 = (bf16[4,3456]{1,0:T(4,128)(2,1)S(1)}, bf16[4,3456]{1,0:T(4,128)(2,1)S(1)}, u32[]{:S(2)}, u32[]{:S(2)}) collective-permute-start(bf16[4,3456]{1,0:T(4,128)(2,1)S(1)} %get-tuple-element.30), channel_id=1, source_target_pairs={{0,5},{1,4},{2,7},{3,6},{4,1},{5,0},{6,3},{7,2},{8,13},{9,12},{10,... | collective-permute-start | bytes 82952 | tf_op jit(solution)/shard_map/ppermute | solution.py:333
  23.9 2.5 %collective-permute-start.13 = (bf16[4,3456]{1,0:T(4,128)(2,1)S(1)}, bf16[4,3456]{1,0:T(4,128)(2,1)S(1)}, u32[]{:S(2)}, u32[]{:S(2)}) collective-permute-start(bf16[4,3456]{1,0:T(4,128)(2,1)S(1)} %get-tuple-element.31), channel_id=1, source_target_pairs={{0,7},{1,6},{2,5},{3,4},{4,3},{5,2},{6,1},{7,0},{8,15},{9,14},{10,... | collective-permute-start | bytes 82952 | tf_op jit(solution)/shard_map/ppermute | solution.py:333
  26.4 0.1 collective-permute-done.12.rest_1_
  26.5 2.5 %collective-permute-done.13.rest_2_ = bf16[4,3456]{1,0:T(4,128)(2,1)S(1)} collective-permute-done((bf16[4,3456]{1,0:T(4,128)(2,1)S(1)}, bf16[4,3456]{1,0:T(4,128)(2,1)S(1)}, u32[]{:S(2)}, u32[]{:S(2)}) %collective-permute-start.13) | collective-permute-done | bytes 27680 | tf_op jit(solution)/shard_map/ppermute | solution.py:333
  29.0 0.7 %shard_map.64 = (f32[4,3328]{1,0:T(4,128)}, f32[1,4]{1,0:T(1,128)}) custom-call(f32[4,3456]{1,0:T(4,128)S(1)} %collective-permute-done.10.near, bf16[4,3456]{1,0:T(4,128)(2,1)S(1)} %collective-permute-done.11.rest_0_, bf16[4,3456]{1,0:T(4,128)(2,1)S(1)} %collective-permute-done.12.rest_1_, bf16[4,3456]{1,0:T(4,128)(2,1)S(1)} %collective-permute-done.13.rest_2_), custom_call_target="tpu_custom_call" | custom-call | tf_op jit(solution)/shard_map/pallas_call | solution.py:303
  (10 shorter events, 0.2 us)
Async XLA Ops:
  0.6 6.6 %collective-permute-start = (bf16[16,3328]{1,0:T(8,128)(2,1)}, bf16[16,3328]{1,0:T(8,128)(2,1)S(1)}, u32[]{:S(2)}, u32[]{:S(2)}) collective-permute-start(bf16[16,3328]{1,0:T(8,128)(2,1)} %bitcast.5), channel_id=1, source_target_pairs={{0,1},{1,0},{2,3},{3,2},{4,5},{5,4},{6,7},{7,6},{8,9},{9,8},{10,11... | collective-permute-start | bytes 319496 | tf_op jit(solution)/shard_map/ppermute | solution.py:333
  1.2 5.5 %collective-permute-start.1 = (s32[2,8,49]{2,1,0:T(8,128)}, s32[2,8,49]{2,1,0:T(8,128)S(1)}, u32[]{:S(2)}, u32[]{:S(2)}) collective-permute-start(s32[2,8,49]{2,1,0:T(8,128)} %bitcast.7), channel_id=1, source_target_pairs={{0,1},{1,0},{2,3},{3,2},{4,5},{5,4},{6,7},{7,6},{8,9},{9,8},{10,11... | collective-permute-start | bytes 9416 | tf_op jit(solution)/shard_map/ppermute | solution.py:333
  1.3 7.4 %collective-permute-start.2 = (bf16[4,3328]{1,0:T(4,128)(2,1)}, bf16[4,3328]{1,0:T(4,128)(2,1)S(1)}, u32[]{:S(2)}, u32[]{:S(2)}) collective-permute-start(bf16[4,3328]{1,0:T(4,128)(2,1)} %bitcast.10), channel_id=1, source_target_pairs={{0,1},{1,0},{2,3},{3,2},{4,5},{5,4},{6,7},{7,6},{8,9},{9,8},{10,11... | collective-permute-start | bytes 79880 | tf_op jit(solution)/shard_map/ppermute | solution.py:333
  1.7 6.9 %collective-permute-start.3 = (bf16[4,3328]{1,0:T(4,128)(2,1)}, bf16[4,3328]{1,0:T(4,128)(2,1)S(1)}, u32[]{:S(2)}, u32[]{:S(2)}) collective-permute-start(bf16[4,3328]{1,0:T(4,128)(2,1)} %bitcast.11), channel_id=1, source_target_pairs={{0,3},{1,2},{2,1},{3,0},{4,7},{5,6},{6,5},{7,4},{8,11},{9,10},{10,... | collective-permute-start | bytes 79880 | tf_op jit(solution)/shard_map/ppermute | solution.py:333
  4.4 4.8 %collective-permute-start.4 = (bf16[4,3328]{1,0:T(4,128)(2,1)}, bf16[4,3328]{1,0:T(4,128)(2,1)S(1)}, u32[]{:S(2)}, u32[]{:S(2)}) collective-permute-start(bf16[4,3328]{1,0:T(4,128)(2,1)} %bitcast.12), channel_id=1, source_target_pairs={{0,5},{1,4},{2,7},{3,6},{4,1},{5,0},{6,3},{7,2},{8,13},{9,12},{10,... | collective-permute-start | bytes 79880 | tf_op jit(solution)/shard_map/ppermute | solution.py:333
  6.7 5.3 %collective-permute-start.5 = (bf16[4,3328]{1,0:T(4,128)(2,1)}, bf16[4,3328]{1,0:T(4,128)(2,1)S(1)}, u32[]{:S(2)}, u32[]{:S(2)}) collective-permute-start(bf16[4,3328]{1,0:T(4,128)(2,1)} %bitcast.13), channel_id=1, source_target_pairs={{0,7},{1,6},{2,5},{3,4},{4,3},{5,2},{6,1},{7,0},{8,15},{9,14},{10,... | collective-permute-start | bytes 79880 | tf_op jit(solution)/shard_map/ppermute | solution.py:333
  12.6 4.5 %collective-permute-start.7 = (s16[256,128]{1,0:T(8,128)(2,1)S(1)}, s16[256,128]{1,0:T(8,128)(2,1)S(1)}, u32[]{:S(2)}, u32[]{:S(2)}) collective-permute-start(s16[256,128]{1,0:T(8,128)(2,1)S(1)} %shard_map.60.refs_0_), channel_id=1, source_target_pairs={{0,16},{8,24},{16,0},{24,8},{1,17},{9,25},{17,1},{25,9},{2,18},{10... | collective-permute-start | bytes 196616 | tf_op jit(solution)/shard_map/ppermute | solution.py:333
  14.2 5.5 %collective-permute-start.8 = (s16[256,128]{1,0:T(8,128)(2,1)S(1)}, s16[256,128]{1,0:T(8,128)(2,1)S(1)}, u32[]{:S(2)}, u32[]{:S(2)}) collective-permute-start(s16[256,128]{1,0:T(8,128)(2,1)S(1)} %shard_map.60.refs_0_), channel_id=1, source_target_pairs={{0,24},{8,16},{16,8},{24,0},{1,25},{9,17},{17,9},{25,1},{2,26},{10... | collective-permute-start | bytes 196616 | tf_op jit(solution)/shard_map/ppermute | solution.py:333
  15.7 4.3 %collective-permute-start.6 = (s16[256,128]{1,0:T(8,128)(2,1)S(1)}, s16[256,128]{1,0:T(8,128)(2,1)S(1)}, u32[]{:S(2)}, u32[]{:S(2)}) collective-permute-start(s16[256,128]{1,0:T(8,128)(2,1)S(1)} %shard_map.60.refs_0_), channel_id=1, source_target_pairs={{0,8},{8,0},{16,24},{24,16},{1,9},{9,1},{17,25},{25,17},{2,10},{10... | collective-permute-start | bytes 196616 | tf_op jit(solution)/shard_map/ppermute | solution.py:333
  20.2 1.2 %collective-permute-start.9 = (f32[32,128]{1,0:T(8,128)S(1)}, f32[32,128]{1,0:T(8,128)S(1)}, u32[]{:S(2)}, u32[]{:S(2)}) collective-permute-start(f32[32,128]{1,0:T(8,128)S(1)} %get-tuple-element.27.own_stats), channel_id=1, source_target_pairs={{0,1},{1,0},{2,3},{3,2},{4,5},{5,4},{6,7},{7,6},{8,9},{9,8},{10,11... | collective-permute-start | bytes 49160 | tf_op jit(solution)/shard_map/ppermute | solution.py:333
  22.1 6.9 %collective-permute-start.10 = (f32[4,3456]{1,0:T(4,128)S(1)}, f32[4,3456]{1,0:T(4,128)S(1)}, u32[]{:S(2)}, u32[]{:S(2)}) collective-permute-start(f32[4,3456]{1,0:T(4,128)S(1)} %get-tuple-element.28), channel_id=1, source_target_pairs={{0,1},{1,0},{2,3},{3,2},{4,5},{5,4},{6,7},{7,6},{8,9},{9,8},{10,11... | collective-permute-start | bytes 165896 | tf_op jit(solution)/shard_map/ppermute | solution.py:333
  22.3 4.1 %collective-permute-start.11 = (bf16[4,3456]{1,0:T(4,128)(2,1)S(1)}, bf16[4,3456]{1,0:T(4,128)(2,1)S(1)}, u32[]{:S(2)}, u32[]{:S(2)}) collective-permute-start(bf16[4,3456]{1,0:T(4,128)(2,1)S(1)} %get-tuple-element.29), channel_id=1, source_target_pairs={{0,3},{1,2},{2,1},{3,0},{4,7},{5,6},{6,5},{7,4},{8,11},{9,10},{10,... | collective-permute-start | bytes 82952 | tf_op jit(solution)/shard_map/ppermute | solution.py:333
  22.3 4.2 %collective-permute-start.12 = (bf16[4,3456]{1,0:T(4,128)(2,1)S(1)}, bf16[4,3456]{1,0:T(4,128)(2,1)S(1)}, u32[]{:S(2)}, u32[]{:S(2)}) collective-permute-start(bf16[4,3456]{1,0:T(4,128)(2,1)S(1)} %get-tuple-element.30), channel_id=1, source_target_pairs={{0,5},{1,4},{2,7},{3,6},{4,1},{5,0},{6,3},{7,2},{8,13},{9,12},{10,... | collective-permute-start | bytes 82952 | tf_op jit(solution)/shard_map/ppermute | solution.py:333
  23.9 5.1 %collective-permute-start.13 = (bf16[4,3456]{1,0:T(4,128)(2,1)S(1)}, bf16[4,3456]{1,0:T(4,128)(2,1)S(1)}, u32[]{:S(2)}, u32[]{:S(2)}) collective-permute-start(bf16[4,3456]{1,0:T(4,128)(2,1)S(1)} %get-tuple-element.31), channel_id=1, source_target_pairs={{0,7},{1,6},{2,5},{3,4},{4,3},{5,2},{6,1},{7,0},{8,15},{9,14},{10,... | collective-permute-start | bytes 82952 | tf_op jit(solution)/shard_map/ppermute | solution.py:333
